TPU v7x, 32 devices: a whole 2x2x4 slice. The times are simulated.
32 devices in a mesh: dp: 8 (over y, x, core), tp: 4 (over z).
Axes of the slice: x: 2, y: 2, z: 4, core: 2. Of those that a mesh axis runs over, the one named last changes fastest.
Arguments:
- tokens: bfloat16 [32768, 512], P(('dp', 'tp')), may hold values from -6 to 6
- cotangent: bfloat16 [32768, 512], P(('dp', 'tp')), may hold values from -12 to 12
- head_choice: int32 [32768, 8], P(('dp', 'tp')), may hold values from 0 to 23, all different within a row
- segment_ids: int32 [32, 1024], P(('dp', 'tp')), may hold values from 0 to 3, never falling along the last dimension, each value on 1 to 512 neighbouring positions
- query_weight: float32 [2, 512, 1536], P(None, 'dp', 'tp'), may hold values from -0.25 to 0.25
- output_weight: float32 [2, 512, 1536], P(None, 'dp', 'tp'), may hold values from -6 to 6
- up_weight: float32 [2, 512, 2048], P(None, 'dp', 'tp'), may hold values from -0.25 to 0.25
- down_weight: float32 [2, 512, 2048], P(None, 'dp', 'tp'), may hold values from -0.25 to 0.25
- keyval_weight: float32 [2, 512, 128], P(None, ('dp', 'tp')), may hold values from -0.25 to 0.25
- router_weight: float32 [2, 512, 24], P(None, ('dp', 'tp')), may hold values from -0.3125 to 0.3125
- norm_gains: float32 [2, 2, 512], P(None, None, ('dp', 'tp')), may hold values from 0.32 to 3
- first_query: float32 [2, 512, 1536], P(None, 'dp', 'tp'), may hold values from -1.5258789e-05 to 1.5258789e-05
- first_output: float32 [2, 512, 1536], P(None, 'dp', 'tp'), may hold values from -7.1525574e-07 to 7.1525574e-07
- first_up: float32 [2, 512, 2048], P(None, 'dp', 'tp'), may hold values from -5.340576e-05 to 5.340576e-05
- first_down: float32 [2, 512, 2048], P(None, 'dp', 'tp'), may hold values from -1.9073486e-05 to 1.9073486e-05
- first_keyval: float32 [2, 512, 128], P(None, ('dp', 'tp')), may hold values from -3.0517578e-05 to 3.0517578e-05
- first_router: float32 [2, 512, 24], P(None, ('dp', 'tp')), may hold values from -3.0517578e-05 to 3.0517578e-05
- first_gains: float32 [2, 2, 512], P(None, None, ('dp', 'tp')), may hold values from -3.0517578e-05 to 3.0517578e-05
- second_query: float32 [2, 512, 1536], P(None, 'dp', 'tp'), may hold values from 4.387996e-12 to 1.7538646e-11
- second_output: float32 [2, 512, 1536], P(None, 'dp', 'tp'), may hold values from 1.0936646e-14 to 4.387996e-14
- second_up: float32 [2, 512, 2048], P(None, 'dp', 'tp'), may hold values from 5.068202e-11 to 2.0272808e-10
- second_down: float32 [2, 512, 2048], P(None, 'dp', 'tp'), may hold values from 8.602606e-12 to 3.4410422e-11
- second_keyval: float32 [2, 512, 128], P(None, ('dp', 'tp')), may hold values from 1.7551984e-11 to 7.0154584e-11
- second_router: float32 [2, 512, 24], P(None, ('dp', 'tp')), may hold values from 1.7551984e-11 to 7.0154584e-11
- second_gains: float32 [2, 2, 512], P(None, None, ('dp', 'tp')), may hold values from 1.7551984e-11 to 7.0154584e-11
- average_query: float32 [2, 512, 1536], P(None, 'dp', 'tp'), may hold values from -0.25 to 0.25
- average_output: float32 [2, 512, 1536], P(None, 'dp', 'tp'), may hold values from -6 to 6
- average_up: float32 [2, 512, 2048], P(None, 'dp', 'tp'), may hold values from -0.25 to 0.25
- average_down: float32 [2, 512, 2048], P(None, 'dp', 'tp'), may hold values from -0.25 to 0.25
- average_keyval: float32 [2, 512, 128], P(None, ('dp', 'tp')), may hold values from -0.25 to 0.25
- average_router: float32 [2, 512, 24], P(None, ('dp', 'tp')), may hold values from -0.3125 to 0.3125
- average_gains: float32 [2, 2, 512], P(None, None, ('dp', 'tp')), may hold values from 0.1 to 3
Outputs:
- layer_out: bfloat16 [32768, 512], P(('dp', 'tp'))
- input_grad: float32 [32768, 512], P(('dp', 'tp'))
- grad_norm: float32 [], replicated
- new_query: float32 [2, 512, 1536], P(None, 'dp', 'tp')
- new_first_query: float32 [2, 512, 1536], P(None, 'dp', 'tp')
- new_second_query: float32 [2, 512, 1536], P(None, 'dp', 'tp')
- new_average_query: float32 [2, 512, 1536], P(None, 'dp', 'tp')
- new_output: float32 [2, 512, 1536], P(None, 'dp', 'tp')
- new_first_output: float32 [2, 512, 1536], P(None, 'dp', 'tp')
- new_second_output: float32 [2, 512, 1536], P(None, 'dp', 'tp')
- new_average_output: float32 [2, 512, 1536], P(None, 'dp', 'tp')
- new_up: float32 [2, 512, 2048], P(None, 'dp', 'tp')
- new_first_up: float32 [2, 512, 2048], P(None, 'dp', 'tp')
- new_second_up: float32 [2, 512, 2048], P(None, 'dp', 'tp')
- new_average_up: float32 [2, 512, 2048], P(None, 'dp', 'tp')
- new_down: float32 [2, 512, 2048], P(None, 'dp', 'tp')
- new_first_down: float32 [2, 512, 2048], P(None, 'dp', 'tp')
- new_second_down: float32 [2, 512, 2048], P(None, 'dp', 'tp')
- new_average_down: float32 [2, 512, 2048], P(None, 'dp', 'tp')
- new_keyval: float32 [2, 512, 128], P(None, ('dp', 'tp'))
- new_first_keyval: float32 [2, 512, 128], P(None, ('dp', 'tp'))
- new_second_keyval: float32 [2, 512, 128], P(None, ('dp', 'tp'))
- new_average_keyval: float32 [2, 512, 128], P(None, ('dp', 'tp'))
- new_router: float32 [2, 512, 24], P(None, ('dp', 'tp'))
- new_first_router: float32 [2, 512, 24], P(None, ('dp', 'tp'))
- new_second_router: float32 [2, 512, 24], P(None, ('dp', 'tp'))
- new_average_router: float32 [2, 512, 24], P(None, ('dp', 'tp'))
- new_gains: float32 [2, 2, 512], P(None, None, ('dp', 'tp'))
- new_first_gains: float32 [2, 2, 512], P(None, None, ('dp', 'tp'))
- new_second_gains: float32 [2, 2, 512], P(None, None, ('dp', 'tp'))
- new_average_gains: float32 [2, 2, 512], P(None, None, ('dp', 'tp'))
Inputs may be any that keep to these rules, and one draw needn't show every extreme that they name: `head_choice`: each token names 8 different head experts, and every expert is named by some token. `segment_ids`: within a packed row of 1024 tokens the ids never fall; a document covers at most half of a row, and some document covers exactly half.
All inputs are finite; a program needn't handle non-finite values.
Results may differ from a plain program's by a relative error of at most 0.03.
The roundings to bfloat16 on the way count: a program that leaves them out, or rounds other values in their place, can miss the bound.
Values may be sent and summed in bfloat16 or wider, within the bound.
No kernel may reach another device: no remote copies, remote signals or barrier semaphores. Data moves between devices by JAX's collectives and lax.ppermute only.
A program may use at most 320 MiB of HBM per device.

v0:
```python
import jax
import jax.numpy as jnp
from jax import lax
from jax.sharding import PartitionSpec as P

E = 24
H = 64
TOPK = 8
LEN = 1024
LAYERS = 2
STEP = 10


epsilon = 1e-06
clip_bound = 0.05
learn_rates = (0.1, 1.0, 0.1, 0.1, 0.1, 0.1, 0.6)
beta_one = 0.9
beta_two = 0.95
adam_floor = 1e-08
weight_decay = 0.1
ema_decay = 0.7
masked_value = -1e30


def contract(left_op, right_op, left_dim, right_dim):
    return lax.dot_general(
        left_op,
        right_op,
        (((left_dim,), (right_dim,)), ((), ())),
        preferred_element_type=jnp.float32,
    )


def normalize(row_data):
    factor = lax.rsqrt(jnp.mean(row_data * row_data, -1, keepdims=True) + epsilon)
    return (row_data * factor, factor)


def norm_back(upstream, normed, factor, gain):
    scaled = upstream * gain
    inner_dot = jnp.mean(scaled * normed, -1, keepdims=True)
    return (factor * (scaled - normed * inner_dot), jnp.sum(upstream * normed, 0))


def gelu_tanh(values):
    return jax.nn.gelu(values, approximate=True)


def visible(segment_row, row_start, row_count):
    row_pos = row_start + jnp.arange(row_count)
    col_pos = jnp.arange(segment_row.shape[0])
    same_doc = segment_row[row_start : row_start + row_count][:, None] == segment_row[None, :]
    return (col_pos[None, :] <= row_pos[:, None]) & same_doc


def attend_forward(queries, key_rows, value_rows, segments):
    length = queries.shape[1]
    score_scale = queries.shape[3] ** (-0.5)
    step_rows = min(512, length)

    def one_sequence(members):
        query_seq, key_seq, value_seq, segment_row = members
        outputs = []
        totals = []
        for row_start in range(0, length, step_rows):
            query_block = query_seq[row_start : row_start + step_rows]
            scores = (
                jnp.einsum("qeh,kh->eqk", query_block, key_seq, preferred_element_type=jnp.float32)
                * score_scale
            )
            scores = jnp.where(
                visible(segment_row, row_start, step_rows)[None], scores, masked_value
            )
            row_max = jnp.max(scores, -1, keepdims=True)
            powers = jnp.exp(scores - row_max)
            row_sum = jnp.sum(powers, -1, keepdims=True)
            attention = (powers / row_sum).astype(jnp.bfloat16)
            outputs.append(
                jnp.einsum("eqk,kh->qeh", attention, value_seq, preferred_element_type=jnp.float32)
            )
            totals.append(row_max[..., 0] + jnp.log(row_sum[..., 0]))
        return (jnp.concatenate(outputs, 0), jnp.concatenate(totals, 1))

    return lax.map(one_sequence, (queries, key_rows, value_rows, segments))


def attend_backward(queries, key_rows, value_rows, segments, log_sums, grad_heads):
    length = queries.shape[1]
    score_scale = queries.shape[3] ** (-0.5)
    step_rows = min(512, length)

    def one_sequence(members):
        query_seq, key_seq, value_seq, segment_row, log_seq, grad_seq = members
        query_grads = []
        key_grad = jnp.zeros(key_seq.shape, jnp.float32)
        value_grad = jnp.zeros(value_seq.shape, jnp.float32)
        for row_start in range(0, length, step_rows):
            query_block = query_seq[row_start : row_start + step_rows]
            grad_block = grad_seq[row_start : row_start + step_rows]
            scores = (
                jnp.einsum("qeh,kh->eqk", query_block, key_seq, preferred_element_type=jnp.float32)
                * score_scale
            )
            scores = jnp.where(
                visible(segment_row, row_start, step_rows)[None], scores, masked_value
            )
            attention = jnp.exp(scores - log_seq[:, row_start : row_start + step_rows, None])
            grad_attention = jnp.einsum(
                "qeh,kh->eqk", grad_block, value_seq, preferred_element_type=jnp.float32
            )
            row_inner = jnp.sum(attention * grad_attention, -1, keepdims=True)
            grad_scores = (attention * (grad_attention - row_inner)).astype(jnp.bfloat16)
            query_grads.append(
                (
                    jnp.einsum(
                        "eqk,kh->qeh", grad_scores, key_seq, preferred_element_type=jnp.float32
                    )
                    * score_scale
                ).astype(jnp.bfloat16)
            )
            key_grad = (
                key_grad
                + jnp.einsum(
                    "eqk,qeh->kh", grad_scores, query_block, preferred_element_type=jnp.float32
                )
                * score_scale
            )
            value_grad = value_grad + jnp.einsum(
                "eqk,qeh->kh",
                attention.astype(jnp.bfloat16),
                grad_block,
                preferred_element_type=jnp.float32,
            )
        return (jnp.concatenate(query_grads, 0), jnp.concatenate([key_grad, value_grad], -1))

    return lax.map(one_sequence, (queries, key_rows, value_rows, segments, log_sums, grad_heads))


def adamw(weight, moment_one, moment_two, average, grad_full, factor, learn_rate):
    clipped = grad_full * factor
    first_new = beta_one * moment_one + (1.0 - beta_one) * clipped
    second_new = beta_two * moment_two + (1.0 - beta_two) * clipped * clipped
    step_ratio = (
        first_new
        / (1.0 - beta_one**STEP)
        / (jnp.sqrt(second_new / (1.0 - beta_two**STEP)) + adam_floor)
    )
    weight_new = weight - learn_rate * (step_ratio + weight_decay * weight)
    return (weight_new, first_new, second_new, ema_decay * average + (1.0 - ema_decay) * weight_new)


def local(
    tokens,
    cotangent,
    head_choice,
    segment_ids,
    query_weight,
    output_weight,
    up_weight,
    down_weight,
    keyval_weight,
    router_weight,
    norm_gains,
    first_query,
    first_output,
    first_up,
    first_down,
    first_keyval,
    first_router,
    first_gains,
    second_query,
    second_output,
    second_up,
    second_down,
    second_keyval,
    second_router,
    second_gains,
    average_query,
    average_output,
    average_up,
    average_down,
    average_keyval,
    average_router,
    average_gains,
):
    token_total = tokens.shape[0] * lax.axis_size("dp") * lax.axis_size("tp")
    gathered = (
        lax.all_gather(query_weight.astype(jnp.bfloat16), "dp", axis=1, tiled=True),
        lax.all_gather(output_weight.astype(jnp.bfloat16), "dp", axis=1, tiled=True),
        lax.all_gather(up_weight.astype(jnp.bfloat16), "dp", axis=1, tiled=True),
        lax.all_gather(down_weight.astype(jnp.bfloat16), "dp", axis=1, tiled=True),
    )
    attn_whole = (
        lax.all_gather(gathered[0], "tp", axis=2, tiled=True),
        lax.all_gather(gathered[1], "tp", axis=2, tiled=True),
    )
    gathered = (attn_whole[0], attn_whole[1], gathered[2], gathered[3])
    query_all, output_all, up_all, down_all = gathered
    shared = (
        lax.all_gather(keyval_weight, ("dp", "tp"), axis=1, tiled=True),
        lax.all_gather(router_weight, ("dp", "tp"), axis=1, tiled=True),
        lax.all_gather(norm_gains, ("dp", "tp"), axis=2, tiled=True),
    )
    keyval_all = shared[0].astype(jnp.bfloat16)
    router_all = shared[1].astype(jnp.bfloat16)
    gains_all = shared[2]
    seq_count = segment_ids.shape[0]
    local_rows = seq_count * LEN
    onehot_full = (head_choice[:, :, None] == jnp.arange(E)[None, None, :]).astype(jnp.float32)
    onehot_low = onehot_full.astype(jnp.bfloat16)
    select = jnp.sum(onehot_full, 1)
    slot_index = head_choice[:, :, None]
    residual = tokens.astype(jnp.float32)
    stored = []
    for depth in range(LAYERS):
        gain_attn = gains_all[depth, 0]
        gain_ffn = gains_all[depth, 1]
        normed, norm_factor = normalize(residual)
        act_rows = (normed * gain_attn).astype(jnp.bfloat16)
        logits = jnp.dot(act_rows, router_all[depth], preferred_element_type=jnp.float32)
        powers = select * jnp.exp(logits - jnp.max(logits, -1, keepdims=True))
        gate_probs = powers / jnp.sum(powers, -1, keepdims=True)
        gate_pick = jnp.take_along_axis(
            gate_probs.astype(jnp.bfloat16), head_choice, axis=1
        ).astype(jnp.float32)
        keyval = jnp.dot(act_rows, keyval_all[depth], preferred_element_type=jnp.float32).astype(
            jnp.bfloat16
        )
        queries_full = jnp.dot(
            act_rows, query_all[depth], preferred_element_type=jnp.float32
        ).reshape(local_rows, E, H)
        picked = (
            jnp.take_along_axis(queries_full, slot_index, axis=1)
            .astype(jnp.bfloat16)
            .reshape(seq_count, LEN, TOPK, H)
        )
        keyval_seq = keyval.reshape(seq_count, LEN, 2 * H)
        key_rows = keyval_seq[:, :, :H]
        value_rows = keyval_seq[:, :, H:]
        heads_out, log_sums = attend_forward(picked, key_rows, value_rows, segment_ids)
        heads_out = heads_out.reshape(local_rows, TOPK, H)
        mixed_heads = (gate_pick[:, :, None] * heads_out).astype(jnp.bfloat16)
        spread = (
            jnp.einsum("tke,tkh->teh", onehot_low, mixed_heads, preferred_element_type=jnp.float32)
            .astype(jnp.bfloat16)
            .reshape(local_rows, E * H)
        )
        branch = contract(spread, output_all[depth], 1, 1)
        after_attn = residual + branch
        normed_ffn, factor_ffn = normalize(after_attn)
        act_ffn = (normed_ffn * gain_ffn).astype(jnp.bfloat16)
        group_ffn = lax.all_gather(act_ffn, "tp", axis=0, tiled=True)
        pre_act = jnp.dot(group_ffn, up_all[depth], preferred_element_type=jnp.float32)
        hidden = gelu_tanh(pre_act).astype(jnp.bfloat16)
        ffn_out = contract(hidden, down_all[depth], 1, 1)
        ffn_out = lax.psum_scatter(ffn_out, "tp", scatter_dimension=0, tiled=True)
        stored.append(
            (
                normed,
                norm_factor,
                act_rows,
                gate_probs,
                gate_pick,
                picked,
                key_rows,
                value_rows,
                heads_out,
                log_sums,
                spread,
                normed_ffn,
                factor_ffn,
                group_ffn,
                pre_act,
                hidden,
            )
        )
        residual = after_attn + ffn_out
    layer_out = residual.astype(jnp.bfloat16)
    upstream = cotangent.astype(jnp.float32)
    list_query = []
    list_output = []
    list_up = []
    list_down = []
    list_keyval = []
    list_router = []
    list_gains = []
    for depth in reversed(range(LAYERS)):
        (
            normed,
            norm_factor,
            act_rows,
            gate_probs,
            gate_pick,
            picked,
            key_rows,
            value_rows,
            heads_out,
            log_sums,
            spread,
            normed_ffn,
            factor_ffn,
            group_ffn,
            pre_act,
            hidden,
        ) = stored[depth]
        gain_attn = gains_all[depth, 0]
        gain_ffn = gains_all[depth, 1]
        grad_rows = lax.all_gather(upstream.astype(jnp.bfloat16), "tp", axis=0, tiled=True)
        grad_down = contract(grad_rows, hidden, 0, 0)
        grad_hidden = jnp.dot(grad_rows, down_all[depth], preferred_element_type=jnp.float32)
        gelu_pull = jax.vjp(gelu_tanh, pre_act)[1]
        grad_pre = gelu_pull(grad_hidden)[0].astype(jnp.bfloat16)
        grad_up = contract(group_ffn, grad_pre, 0, 0)
        grad_group_ffn = contract(grad_pre, up_all[depth], 1, 1)
        grad_act_ffn = lax.psum_scatter(grad_group_ffn, "tp", scatter_dimension=0, tiled=True)
        grad_normed_ffn, grad_gain_ffn = norm_back(grad_act_ffn, normed_ffn, factor_ffn, gain_ffn)
        upstream = upstream + grad_normed_ffn
        attn_rows_low = upstream.astype(jnp.bfloat16)
        grad_output = contract(attn_rows_low, spread, 0, 0)
        grad_spread = jnp.dot(
            attn_rows_low, output_all[depth], preferred_element_type=jnp.float32
        ).reshape(local_rows, E, H)
        grad_mixed = jnp.take_along_axis(grad_spread, slot_index, axis=1)
        grad_gate_slot = jnp.sum(grad_mixed * heads_out, -1)
        grad_heads = (
            (gate_pick[:, :, None] * grad_mixed)
            .astype(jnp.bfloat16)
            .reshape(seq_count, LEN, TOPK, H)
        )
        grad_picked, grad_keyval = attend_backward(
            picked, key_rows, value_rows, segment_ids, log_sums, grad_heads
        )
        grad_picked = grad_picked.reshape(local_rows, TOPK, H)
        grad_queries = (
            jnp.einsum("tke,tkh->teh", onehot_low, grad_picked, preferred_element_type=jnp.float32)
            .astype(jnp.bfloat16)
            .reshape(local_rows, E * H)
        )
        grad_query = contract(act_rows, grad_queries, 0, 0)
        grad_act = contract(grad_queries, query_all[depth], 1, 1)
        grad_gates = jnp.sum(onehot_full * grad_gate_slot[:, :, None], 1)
        grad_kv_low = grad_keyval.reshape(local_rows, 2 * H).astype(jnp.bfloat16)
        grad_keyval_w = contract(act_rows, grad_kv_low, 0, 0)
        grad_act = grad_act + contract(grad_kv_low, keyval_all[depth], 1, 1)
        grad_logits = gate_probs * (
            grad_gates - jnp.sum(gate_probs * grad_gates, -1, keepdims=True)
        )
        grad_logit_low = grad_logits.astype(jnp.bfloat16)
        grad_router = contract(act_rows, grad_logit_low, 0, 0)
        grad_act = grad_act + contract(grad_logit_low, router_all[depth], 1, 1)
        grad_normed, grad_gain_attn = norm_back(grad_act, normed, norm_factor, gain_attn)
        upstream = upstream + grad_normed
        list_query.insert(0, grad_query)
        list_output.insert(0, grad_output)
        list_up.insert(0, grad_up)
        list_down.insert(0, grad_down)
        list_keyval.insert(0, grad_keyval_w)
        list_router.insert(0, grad_router)
        list_gains.insert(0, jnp.stack([grad_gain_attn, grad_gain_ffn]))
    mean_scale = 1.0 / token_total
    big_terms = (
        jnp.stack(list_query) * mean_scale,
        jnp.stack(list_output) * mean_scale,
        jnp.stack(list_up) * mean_scale,
        jnp.stack(list_down) * mean_scale,
    )
    attn_terms = (
        lax.psum_scatter(big_terms[0], "tp", scatter_dimension=2, tiled=True),
        lax.psum_scatter(big_terms[1], "tp", scatter_dimension=2, tiled=True),
    )
    big_terms = (attn_terms[0], attn_terms[1], big_terms[2], big_terms[3])
    sum_query, sum_output, sum_up, sum_down = (
        lax.psum_scatter(big_terms[0], "dp", scatter_dimension=1, tiled=True),
        lax.psum_scatter(big_terms[1], "dp", scatter_dimension=1, tiled=True),
        lax.psum_scatter(big_terms[2], "dp", scatter_dimension=1, tiled=True),
        lax.psum_scatter(big_terms[3], "dp", scatter_dimension=1, tiled=True),
    )
    sum_keyval, sum_router, sum_gains = (
        lax.psum_scatter(
            jnp.stack(list_keyval) * mean_scale, ("dp", "tp"), scatter_dimension=1, tiled=True
        ),
        lax.psum_scatter(
            jnp.stack(list_router) * mean_scale, ("dp", "tp"), scatter_dimension=1, tiled=True
        ),
        lax.psum_scatter(
            jnp.stack(list_gains) * mean_scale, ("dp", "tp"), scatter_dimension=2, tiled=True
        ),
    )
    reduced = (sum_query, sum_output, sum_up, sum_down, sum_keyval, sum_router, sum_gains)
    local_squares = jnp.sum(jnp.stack([jnp.sum(entry_grad * entry_grad) for entry_grad in reduced]))
    grad_norm = jnp.sqrt(lax.psum(local_squares, ("dp", "tp")))
    factor = jnp.minimum(1.0, clip_bound / grad_norm)
    update_query = adamw(
        query_weight, first_query, second_query, average_query, sum_query, factor, learn_rates[0]
    )
    update_output = adamw(
        output_weight,
        first_output,
        second_output,
        average_output,
        sum_output,
        factor,
        learn_rates[1],
    )
    update_up = adamw(up_weight, first_up, second_up, average_up, sum_up, factor, learn_rates[2])
    update_down = adamw(
        down_weight, first_down, second_down, average_down, sum_down, factor, learn_rates[3]
    )
    update_keyval = adamw(
        keyval_weight,
        first_keyval,
        second_keyval,
        average_keyval,
        sum_keyval,
        factor,
        learn_rates[4],
    )
    update_router = adamw(
        router_weight,
        first_router,
        second_router,
        average_router,
        sum_router,
        factor,
        learn_rates[5],
    )
    update_gains = adamw(
        norm_gains, first_gains, second_gains, average_gains, sum_gains, factor, learn_rates[6]
    )
    return (
        layer_out,
        upstream,
        grad_norm,
        update_query[0],
        update_query[1],
        update_query[2],
        update_query[3],
        update_output[0],
        update_output[1],
        update_output[2],
        update_output[3],
        update_up[0],
        update_up[1],
        update_up[2],
        update_up[3],
        update_down[0],
        update_down[1],
        update_down[2],
        update_down[3],
        update_keyval[0],
        update_keyval[1],
        update_keyval[2],
        update_keyval[3],
        update_router[0],
        update_router[1],
        update_router[2],
        update_router[3],
        update_gains[0],
        update_gains[1],
        update_gains[2],
        update_gains[3],
    )


def solution(mesh):
    in_specs = (
        P(("dp", "tp"), None),
        P(("dp", "tp"), None),
        P(("dp", "tp"), None),
        P(("dp", "tp"), None),
        P(None, "dp", "tp"),
        P(None, "dp", "tp"),
        P(None, "dp", "tp"),
        P(None, "dp", "tp"),
        P(None, ("dp", "tp"), None),
        P(None, ("dp", "tp"), None),
        P(None, None, ("dp", "tp")),
        P(None, "dp", "tp"),
        P(None, "dp", "tp"),
        P(None, "dp", "tp"),
        P(None, "dp", "tp"),
        P(None, ("dp", "tp"), None),
        P(None, ("dp", "tp"), None),
        P(None, None, ("dp", "tp")),
        P(None, "dp", "tp"),
        P(None, "dp", "tp"),
        P(None, "dp", "tp"),
        P(None, "dp", "tp"),
        P(None, ("dp", "tp"), None),
        P(None, ("dp", "tp"), None),
        P(None, None, ("dp", "tp")),
        P(None, "dp", "tp"),
        P(None, "dp", "tp"),
        P(None, "dp", "tp"),
        P(None, "dp", "tp"),
        P(None, ("dp", "tp"), None),
        P(None, ("dp", "tp"), None),
        P(None, None, ("dp", "tp")),
    )
    out_specs = (
        P(("dp", "tp"), None),
        P(("dp", "tp"), None),
        P(),
        P(None, "dp", "tp"),
        P(None, "dp", "tp"),
        P(None, "dp", "tp"),
        P(None, "dp", "tp"),
        P(None, "dp", "tp"),
        P(None, "dp", "tp"),
        P(None, "dp", "tp"),
        P(None, "dp", "tp"),
        P(None, "dp", "tp"),
        P(None, "dp", "tp"),
        P(None, "dp", "tp"),
        P(None, "dp", "tp"),
        P(None, "dp", "tp"),
        P(None, "dp", "tp"),
        P(None, "dp", "tp"),
        P(None, "dp", "tp"),
        P(None, ("dp", "tp"), None),
        P(None, ("dp", "tp"), None),
        P(None, ("dp", "tp"), None),
        P(None, ("dp", "tp"), None),
        P(None, ("dp", "tp"), None),
        P(None, ("dp", "tp"), None),
        P(None, ("dp", "tp"), None),
        P(None, ("dp", "tp"), None),
        P(None, None, ("dp", "tp")),
        P(None, None, ("dp", "tp")),
        P(None, None, ("dp", "tp")),
        P(None, None, ("dp", "tp")),
    )
    return jax.shard_map(local, mesh=mesh, in_specs=in_specs, out_specs=out_specs, check_vma=False)
```

profile of v0, /device:TPU:0, one launch (start us, length us, event | category | flops | bytes accessed | tf_op | source)
XLA Modules:
  0.0 2998.8 jit_solution(10652531029692790986)
XLA Ops:
  35.7 73.3 %all_gather.40 = bf16[2,512,24]{2,1,0:T(8,128)(2,1)S(1)} all-gather(bf16[2,16,24]{2,1,0:T(8,128)(2,1)S(1)} %convert.21), channel_id=1, replica_groups=mesh['dp'=8,'tp'=4] {'dp','tp'}, dimensions={1}, use_global_device_ids=true | all-gather | bytes 50688 | tf_op jit(solution)/shard_map/all_gather | solution.py:201
  109.0 68.4 %all_gather.41 = bf16[2,512,128]{2,1,0:T(8,128)(2,1)S(1)} all-gather(bf16[2,16,128]{2,1,0:T(8,128)(2,1)S(1)} %convert.20), channel_id=1, replica_groups=mesh['dp'=8,'tp'=4] {'dp','tp'}, dimensions={1}, use_global_device_ids=true | all-gather | bytes 270336 | tf_op jit(solution)/shard_map/all_gather | solution.py:200
  177.8 69.4 %all_gather.39 = f32[2,2,512]{1,0,2:T(2,128)S(1)} all-gather(f32[2,2,16]{1,0,2:T(2,128)S(1)} %copy.373), channel_id=1, replica_groups=mesh['dp'=8,'tp'=4] {'dp','tp'}, dimensions={2}, use_global_device_ids=true | all-gather | bytes 8448 | tf_op jit(solution)/shard_map/all_gather | solution.py:202
  263.5 68.7 %gather_fusion = bf16[8192]{0:T(1024)(128)(2,1)S(1)} fusion(bf16[1024,24]{0,1:T(8,128)(2,1)S(1)} %get-tuple-element.334, s32[8192]{0:T(1024)S(1)} %reshape.382), kind=kCustom, calls=%fused_computation.clone | custom fusion | bytes 98304 | tf_op jit(solution)/shard_map/jit(take_along_axis)/gather | solution.py:223
  353.1 98.1 %gather_fusion.1 = bf16[8192,64]{1,0:T(8,128)(2,1)S(1)} fusion(bf16[1024,24,64]{2,1,0:T(8,128)(2,1)} %copy.380, s32[8192]{0:T(1024)S(1)} %reshape.386), kind=kCustom, calls=%fused_computation.1.clone | custom fusion | bytes 2162688 | tf_op jit(solution)/shard_map/jit(take_along_axis)/gather | solution.py:233
  528.5 77.7 %all-gather.13.cloned.1.call-done = bf16[4096,512]{0,1:T(8,128)(2,1)} async-done(((bf16[1024,512]{0,1:T(8,128)(2,1)}), bf16[4096,512]{0,1:T(8,128)(2,1)}) %all-gather.13.cloned.1.call-update) | async-done | bytes 4194320 | tf_op jit(solution)/shard_map/all_gather | solution.py:252
  643.4 141.8 %reduce-scatter.15.cloned.1.call-done = f32[1024,512]{0,1:T(8,128)} async-done(((f32[4096,512]{0,1:T(8,128)}), f32[1024,512]{0,1:T(8,128)}) %reduce-scatter.15.cloned.1.call-update) | async-done | bytes 2097168 | tf_op jit(solution)/shard_map/reduce_scatter | solution.py:256
  801.2 98.4 %gather_fusion.3 = bf16[8192,64]{1,0:T(8,128)(2,1)S(1)} fusion(bf16[1024,24,64]{2,1,0:T(8,128)(2,1)} %copy.393, s32[8192]{0:T(1024)S(1)} %reshape.386), kind=kCustom, calls=%fused_computation.3.clone | custom fusion | bytes 2162688 | tf_op jit(solution)/shard_map/jit(take_along_axis)/gather | solution.py:233
  918.7 68.7 %gather_fusion.2 = bf16[8192]{0:T(1024)(128)(2,1)S(1)} fusion(bf16[1024,24]{0,1:T(8,128)(2,1)S(1)} %get-tuple-element.328, s32[8192]{0:T(1024)S(1)} %reshape.382), kind=kCustom, calls=%fused_computation.2.clone | custom fusion | bytes 98304 | tf_op jit(solution)/shard_map/jit(take_along_axis)/gather | solution.py:223
  1047.5 80.5 %all-gather.19.cloned.1.call-done = bf16[4096,512]{0,1:T(8,128)(2,1)} async-done(((bf16[1024,512]{0,1:T(8,128)(2,1)}), bf16[4096,512]{0,1:T(8,128)(2,1)}) %all-gather.19.cloned.1.call-update) | async-done | bytes 4194320 | tf_op jit(solution)/shard_map/all_gather | solution.py:252
  1136.0 72.9 %all-gather.21.cloned.1.call-done = bf16[4096,512]{1,0:T(8,128)(2,1)} async-done(((bf16[1024,512]{1,0:T(8,128)(2,1)}), bf16[4096,512]{1,0:T(8,128)(2,1)}) %all-gather.21.cloned.1.call-update) | async-done | bytes 4194320 | tf_op jit(solution)/shard_map/all_gather | solution.py:308
  1246.1 123.7 %reduce-scatter.19.cloned.1.call-done = f32[1024,512]{0,1:T(8,128)} async-done(((f32[4096,512]{0,1:T(8,128)}), f32[1024,512]{0,1:T(8,128)}) %reduce-scatter.19.cloned.1.call-update) | async-done | bytes 2097168 | tf_op jit(solution)/shard_map/reduce_scatter | solution.py:315
  1372.5 144.7 %reduce-scatter.17.cloned.1.call-done = f32[1024,512]{0,1:T(8,128)} async-done(((f32[4096,512]{0,1:T(8,128)}), f32[1024,512]{0,1:T(8,128)}) %reduce-scatter.17.cloned.1.call-update) | async-done | bytes 2097168 | tf_op jit(solution)/shard_map/reduce_scatter | solution.py:256
  1536.9 119.2 %gather_fusion.4 = f32[8192,64]{1,0:T(8,128)} fusion(f32[1024,24,64]{2,1,0:T(8,128)} %copy.405, s32[8192]{0:T(1024)S(1)} %copy-done.1), kind=kCustom, calls=%fused_computation.4.clone | custom fusion | bytes 4259840 | tf_op jit(solution)/shard_map/jit(take_along_axis)/gather | solution.py:323
  1762.8 81.7 %all-gather.23.cloned.1.call-done = bf16[4096,512]{0,1:T(8,128)(2,1)} async-done(((bf16[1024,512]{0,1:T(8,128)(2,1)}), bf16[4096,512]{0,1:T(8,128)(2,1)}) %all-gather.23.cloned.1.call-update) | async-done | bytes 4194320 | tf_op jit(solution)/shard_map/all_gather | solution.py:308
  1868.9 136.9 %reduce-scatter.21.cloned.1.call-done = f32[1024,512]{0,1:T(8,128)} async-done(((f32[4096,512]{0,1:T(8,128)}), f32[1024,512]{0,1:T(8,128)}) %reduce-scatter.21.cloned.1.call-update) | async-done | bytes 2097168 | tf_op jit(solution)/shard_map/reduce_scatter | solution.py:315
  2039.6 119.6 %gather_fusion.5 = f32[8192,64]{1,0:T(8,128)} fusion(f32[1024,24,64]{2,1,0:T(8,128)} %copy.425, s32[8192]{0:T(1024)S(1)} %copy-done.1), kind=kCustom, calls=%fused_computation.5.clone | custom fusion | bytes 4259840 | tf_op jit(solution)/shard_map/jit(take_along_axis)/gather | solution.py:323
  2360.6 43.5 %reduce-scatter.33.cloned.1.call-done = f32[2,64,512]{2,1,0:T(8,128)} async-done(((f32[2,512,512]{2,1,0:T(8,128)}), f32[2,64,512]{2,1,0:T(8,128)}) %reduce-scatter.33.cloned.1.call-update) | async-done | bytes 262160 | tf_op jit(solution)/shard_map/reduce_scatter | solution.py:376
  2405.7 43.1 %reduce-scatter.31.cloned.1.call-done = f32[2,64,512]{2,1,0:T(8,128)} async-done(((f32[2,512,512]{2,1,0:T(8,128)}), f32[2,64,512]{2,1,0:T(8,128)}) %reduce-scatter.31.cloned.1.call-update) | async-done | bytes 262160 | tf_op jit(solution)/shard_map/reduce_scatter | solution.py:375
  2454.6 130.3 %reduce-scatter.37.cloned.1.call-done = f32[16,4]{1,0:T(8,128)} async-done(((f32[512,4]{1,0:T(8,128)}), f32[16,4]{1,0:T(8,128)}) %reduce-scatter.37.cloned.1.call-update) | async-done | bytes 272
  2586.4 129.1 %all-reduce.3.cloned.1.call-done = f32[2,512,24]{2,0,1:T(2,128)} async-done(((f32[2,512,24]{2,0,1:T(2,128)}), f32[2,512,24]{2,0,1:T(2,128)}) %all-reduce.3.cloned.1.call-update) | async-done | bytes 98320
  2716.9 134.4 %reduce-scatter.35.cloned.1.call-done = f32[2,16,128]{2,1,0:T(8,128)} async-done(((f32[2,512,128]{2,1,0:T(8,128)}), f32[2,16,128]{2,1,0:T(8,128)}) %reduce-scatter.35.cloned.1.call-update) | async-done | bytes 16400 | tf_op jit(solution)/shard_map/reduce_scatter | solution.py:379
  2891.0 40.5 %reduce-scatter.25.cloned.1.call-done = f32[2,64,384]{2,1,0:T(8,128)} async-done(((f32[2,512,384]{2,1,0:T(8,128)}), f32[2,64,384]{2,1,0:T(8,128)}) %reduce-scatter.25.cloned.1.call-update) | async-done | bytes 196624 | tf_op jit(solution)/shard_map/reduce_scatter | solution.py:373
  2940.7 39.3 %psum.7 = f32[]{:T(128)} all-reduce(f32[]{:T(128)S(6)} %reduce_sum.395), channel_id=1, replica_groups=mesh['dp'=8,'tp'=4] {'dp','tp'}, use_global_device_ids=true, to_apply=%region_55.58 | all-reduce | flops 1 | bytes 8 | tf_op jit(solution)/shard_map/psum | solution.py:391
  (562 shorter events, 771.9 us)
Async XLA Ops:
  7.3 328.2 %all-gather.9.cloned.1.call-start = ((), (), s32[]{:S(2)}) async-start(), calls=%async_computation.12 | async-start | bytes 3932160 | tf_op jit(solution)/shard_map/all_gather | solution.py:194
  21.2 501.0 %all-gather.11.cloned.1.call-start = ((), (), s32[]{:S(2)}) async-start(), calls=%async_computation.13 | async-start | bytes 3932160 | tf_op jit(solution)/shard_map/all_gather | solution.py:195
  33.5 495.0 %all-gather.15.cloned.1.call-start = ((), (), s32[]{:S(2)}) async-start(), calls=%async_computation.15 | async-start | bytes 1179648 | tf_op jit(solution)/shard_map/all_gather | solution.py:190
  35.2 571.0 %all-gather.13.cloned.1.call-start = ((), (), s32[]{:S(2)}) async-start(), calls=%async_computation.14 | async-start | bytes 5242880 | tf_op jit(solution)/shard_map/all_gather | solution.py:252
  35.3 866.6 %copy-start.94 = (pred[1024,8]{0,1:T(8,128)(4,1)}, pred[1024,8]{0,1:T(8,128)(4,1)S(1)}, u32[]{:S(2)}) copy-start(pred[1024,8]{0,1:T(8,128)(4,1)S(1)} %and_bitcast_fusion) | copy-start | bytes 24580
  260.6 540.6 %copy-start = (s32[8192]{0:T(1024)}, s32[8192]{0:T(1024)S(1)}, u32[]{:S(2)}) copy-start(s32[8192]{0:T(1024)S(1)} %reshape.386) | copy-start | bytes 98308
  527.7 102.9 %all-gather.17.cloned.1.call-start = ((), (), s32[]{:S(2)}) async-start(), calls=%async_computation.16 | async-start | bytes 1179648 | tf_op jit(solution)/shard_map/all_gather | solution.py:191
  528.4 256.8 %reduce-scatter.15.cloned.1.call-start = ((), (), s32[]{:S(2)}) async-start(), calls=%async_computation.17 | async-start | bytes 10485760 | tf_op jit(solution)/shard_map/reduce_scatter | solution.py:256
  640.6 487.4 %all-gather.19.cloned.1.call-start = ((), (), s32[]{:S(2)}) async-start(), calls=%async_computation.18 | async-start | bytes 5242880 | tf_op jit(solution)/shard_map/all_gather | solution.py:252
  1046.7 162.2 %all-gather.21.cloned.1.call-start = ((), (), s32[]{:S(2)}) async-start(), calls=%async_computation.20 | async-start | bytes 5242880 | tf_op jit(solution)/shard_map/all_gather | solution.py:308
  1047.4 322.4 %reduce-scatter.19.cloned.1.call-start = ((), (), s32[]{:S(2)}) async-start(), calls=%async_computation.21 | async-start | bytes 10485760 | tf_op jit(solution)/shard_map/reduce_scatter | solution.py:315
  1226.6 290.6 %reduce-scatter.17.cloned.1.call-start = ((), (), s32[]{:S(2)}) async-start(), calls=%async_computation.19 | async-start | bytes 10485760 | tf_op jit(solution)/shard_map/reduce_scatter | solution.py:256
  1236.8 607.8 %all-gather.23.cloned.1.call-start = ((), (), s32[]{:S(2)}) async-start(), calls=%async_computation.22 | async-start | bytes 5242880 | tf_op jit(solution)/shard_map/all_gather | solution.py:308
  1762.7 243.0 %reduce-scatter.21.cloned.1.call-start = ((), (), s32[]{:S(2)}) async-start(), calls=%async_computation.23 | async-start | bytes 10485760 | tf_op jit(solution)/shard_map/reduce_scatter | solution.py:315
  1862.6 461.4 %reduce-scatter.27.cloned.1.call-start = ((), (), s32[]{:S(2)}) async-start(), calls=%async_computation.26 | async-start | bytes 7864320 | tf_op jit(solution)/shard_map/reduce_scatter | solution.py:369
  2016.7 342.5 %reduce-scatter.23.cloned.1.call-start = ((), (), s32[]{:S(2)}) async-start(), calls=%async_computation.24 | async-start | bytes 7864320 | tf_op jit(solution)/shard_map/reduce_scatter | solution.py:368
  2247.6 156.6 %reduce-scatter.33.cloned.1.call-start = ((), (), s32[]{:S(2)}) async-start(), calls=%async_computation.29 | async-start | bytes 2359296 | tf_op jit(solution)/shard_map/reduce_scatter | solution.py:376
  2263.7 185.1 %reduce-scatter.31.cloned.1.call-start = ((), (), s32[]{:S(2)}) async-start(), calls=%async_computation.28 | async-start | bytes 2359296 | tf_op jit(solution)/shard_map/reduce_scatter | solution.py:375
  2275.9 309.0 %reduce-scatter.37.cloned.1.call-start = ((), (), s32[]{:S(2)}) async-start(), calls=%async_computation.31 | async-start | bytes 270336
  2322.0 393.6 %all-reduce.3.cloned.1.call-start = ((), (), s32[]{:S(2)}) async-start(), calls=%async_computation.32 | async-start | bytes 1048576
  2323.1 528.2 %reduce-scatter.35.cloned.1.call-start = ((), (), s32[]{:S(2)}) async-start(), calls=%async_computation.30 | async-start | bytes 540672 | tf_op jit(solution)/shard_map/reduce_scatter | solution.py:379
  2324.0 565.3 %reduce-scatter.29.cloned.1.call-start = ((), (), s32[]{:S(2)}) async-start(), calls=%async_computation.27 | async-start | bytes 1769472 | tf_op jit(solution)/shard_map/reduce_scatter | solution.py:374
  2324.6 606.9 %reduce-scatter.25.cloned.1.call-start = ((), (), s32[]{:S(2)}) async-start(), calls=%async_computation.25 | async-start | bytes 1769472 | tf_op jit(solution)/shard_map/reduce_scatter | solution.py:373
  2454.6 531.6 %copy-start.80 = (f32[2,64,384]{2,1,0:T(8,128)S(1)}, f32[2,64,384]{2,1,0:T(8,128)}, u32[]{:S(2)}) copy-start(f32[2,64,384]{2,1,0:T(8,128)} %param.40) | copy-start | bytes 589828
  (153 other events, 10560.1 us)
Sparse Core Ops, SparseCore 0:
  21.3 67.6 all-gather.8
  90.6 65.9 all-gather.10
  159.0 22.1 all-gather.14
  527.8 78.3 all-gather.12
  608.6 22.0 all-gather.16
  640.8 144.4 reduce-scatter.14
  1046.8 81.1 all-gather.18
  1129.6 79.2 all-gather.20
  1226.7 143.0 reduce-scatter.18
  1372.0 145.1 reduce-scatter.16
  1762.9 81.6 all-gather.22
  1862.7 142.9 reduce-scatter.20
  2016.8 111.4 reduce-scatter.26
  2247.7 111.4 reduce-scatter.22
  2362.3 41.7 reduce-scatter.32
  2407.6 41.2 reduce-scatter.30
  2451.5 133.3 reduce-scatter.36
  2590.9 124.5 all-reduce.2
  2717.8 133.4 reduce-scatter.34
  2854.8 34.5 reduce-scatter.28
  2893.0 38.4 reduce-scatter.24
where the time goes:
time: 3010 us; the launch traced here: 3000 us
  waiting for transfers between devices  1470 us (49%)
  local copies, waits for them, and re-layouts  720 us (24%)
  matrix products  345 us (11%)
  blocking collectives  275 us (9%)
  other arithmetic  165 us (5%)
    reduce_scatter x2, waiting for transfers between devices, local(): ffn_out = lax.psum_scatter(ffn_out, 'tp', scatter_dimension=0, tiled=True)  286 us
    unnamed x23, waiting for transfers between devices  261 us
    reduce_scatter x2, waiting for transfers between devices, local(): lax.psum_scatter(grad_group_ffn, 'tp', scatter_dimension=0, tiled=True)  261 us
    gather x4, local copies, waits for them, and re-layouts, local(): grad_mixed = jnp.take_along_axis(grad_spread, slot_index, axis=1)  246 us
    gather x6, local copies, waits for them, and re-layouts, local(): jnp.take_along_axis(queries_full, slot_index, axis=1).astype(jnp.bfloat16)  201 us
    all_gather x2, waiting for transfers between devices, local(): group_ffn = lax.all_gather(act_ffn, 'tp', axis=0, tiled=True)  158 us
    all_gather x2, waiting for transfers between devices, local(): lax.all_gather(upstream.astype(jnp.bfloat16), 'tp', axis=0, tiled=True)  155 us
    gather x8, local copies, waits for them, and re-layouts, local(): jnp.take_along_axis(gate_probs.astype(jnp.bfloat16), head_choice, axis=1)  139 us
  transfers between devices with their start and end apart: 21, of which 17 were waited for; matrix products, arithmetic and copies ran while one was open for 21% of the time, Pallas kernels for 0%

commit v1 on v0

v1 whole, which is shorter than its diff:
```python
import functools

import jax
import jax.numpy as jnp
from jax import lax
from jax.experimental import pallas as pl
from jax.experimental.pallas import tpu as pltpu
from jax.sharding import PartitionSpec as P

E = 24
H = 64
TOPK = 8
LEN = 1024
LAYERS = 2
STEP = 10
D = 512
FF = 2048
EH = E * H
KH = TOPK * H
PAIRS = TOPK // 2
COLS = EH // 128
ROWS = 256
STEPS = LEN // ROWS
SUB = 128
VDP = 8
VTP = 4
RW = D // VDP
CA = EH // VTP
CF = FF // VTP
RM = D // (VDP * VTP)
RA = 2 * RW + RM
RQ = RW + RM
VMEM = 60 * 1024 * 1024

epsilon = 1e-06
clip_bound = 0.05
learn_rates = (0.1, 1.0, 0.1, 0.1, 0.1, 0.1, 0.6)
beta_one = 0.9
beta_two = 0.95
adam_floor = 1e-08
weight_decay = 0.1
ema_decay = 0.7
masked_value = -1e30
f32 = jnp.float32
bf16 = jnp.bfloat16


def dot(a, b):
    return lax.dot_general(a, b, (((1,), (0,)), ((), ())), preferred_element_type=f32)


def dot_nt(a, b):
    return lax.dot_general(a, b, (((1,), (1,)), ((), ())), preferred_element_type=f32)


def lanes(rows, dtype=jnp.int32):
    return lax.broadcasted_iota(jnp.int32, (rows, 128), 1).astype(dtype)


def normalize(x):
    factor = lax.rsqrt(jnp.mean(x * x, -1, keepdims=True) + epsilon)
    return x * factor, factor


def both_halves(x, low_half):
    turned = pltpu.roll(x, 64, 1)
    return jnp.where(low_half, x, turned), jnp.where(low_half, turned, x)


def slot_columns(hc):
    rows = hc.shape[0]
    return [jnp.broadcast_to(hc[:, k : k + 1], (rows, 128)).astype(bf16) for k in range(TOPK)]


def pick_heads(full, slots):
    rows = full.shape[0]
    low_half = lanes(rows) < 64
    low_half16 = lanes(rows).astype(bf16) < jnp.asarray(64, bf16)
    pairs = [jnp.where(low_half16, slots[2 * p], slots[2 * p + 1]) for p in range(PAIRS)]
    out = [jnp.zeros((rows, 128), bf16) for _ in range(PAIRS)]
    for c in range(COLS):
        even, odd = both_halves(full[:, c * 128 : (c + 1) * 128], low_half)
        even = even.astype(bf16)
        odd = odd.astype(bf16)
        for p in range(PAIRS):
            out[p] = jnp.where(pairs[p] == jnp.asarray(2 * c, bf16), even, out[p])
            out[p] = jnp.where(pairs[p] == jnp.asarray(2 * c + 1, bf16), odd, out[p])
    return out


def spread_heads(pair_values, slots, store):
    rows = pair_values[0].shape[0]
    low_half = lanes(rows) < 64
    copies = []
    for p in range(PAIRS):
        even, odd = both_halves(pair_values[p], low_half)
        copies += [even.astype(bf16), odd.astype(bf16)]
    half = jnp.where(lanes(rows).astype(bf16) < jnp.asarray(64, bf16), jnp.asarray(0, bf16), jnp.asarray(1, bf16))
    for c in range(COLS):
        expert = half + jnp.asarray(2 * c, bf16)
        total = jnp.zeros((rows, 128), bf16)
        for k in range(TOPK):
            total = jnp.where(slots[k] == expert, copies[k], total)
        store(c, total)


def place(refs, scratch, idx, first, count, width):
    stride = refs[0].shape[0] // VTP
    for j in range(VDP):
        row = pl.multiple_of(idx[j] * count, count)
        for q in range(VTP):
            col = pl.multiple_of(idx[VDP + q] * width, 128)
            scratch[pl.ds(row, count), pl.ds(col, width)] = refs[j][
                q * stride + first : q * stride + first + count, :
            ]


def place_misc(refs, scratch, idx, first):
    stride = refs[0].shape[0] // VTP
    for j in range(VDP):
        for q in range(VTP):
            row = pl.multiple_of((idx[j] * VTP + idx[VDP + q]) * RM, RM)
            scratch[pl.ds(row, RM), :] = refs[j][q * stride + first : q * stride + first + RM, :]


def hand_out(keep, send, grad, idx, first, count):
    for j in range(VDP):
        row = pl.multiple_of(idx[j] * count, count)
        target = keep if j % 2 == 0 else send
        target[j // 2, 0, first : first + count, :] = grad[pl.ds(row, count), :].astype(bf16)


def bias_of(segc, segr_ref, row0, start, width):
    rows = row0 + lax.broadcasted_iota(jnp.int32, (SUB, width), 0)
    cols = start + lax.broadcasted_iota(jnp.int32, (SUB, width), 1)
    same = segc[:, 0:1] == segr_ref[0:1, pl.ds(start, width)]
    return jnp.where((cols <= rows) & same, 0.0, masked_value).astype(f32)


def attn_forward_kernel(idx, x_ref, hc_ref, segc_ref, segr_ref, *rest):
    w_refs = rest[:VDP]
    (mid_ref, qs_ref, kv_ref, ho_ref, lse_ref, spread_ref, gate_ref, gsl_ref, gains_ref) = rest[VDP : VDP + 9]
    (wq, wo, misc, gain_s, kt_lo, kt_hi, v_lo, v_hi, qst, mixed_s) = rest[VDP + 9 :]
    step = pl.program_id(0)

    @pl.when(step == 0)
    def _():
        place(w_refs, wq, idx, 0, RW, CA)
        place(w_refs, wo, idx, RW, RW, CA)
        place_misc(w_refs, misc, idx, 2 * RW)
        turned = misc[:, 128:256].astype(f32).T
        gain_s[...] = jnp.zeros_like(gain_s)
        gain_s[0:1, :] = turned[24:25] + turned[25:26] + turned[26:27]
        gain_s[1:2, :] = turned[27:28] + turned[28:29] + turned[29:30]
        gains_ref[...] = gain_s[...]

    x = x_ref[...].astype(f32)
    normed, _ = normalize(x)
    act = (normed * gain_s[0:1, :]).astype(bf16)
    hc = hc_ref[...]
    slots = slot_columns(hc)
    low_half = lanes(ROWS) < 64
    lane = lanes(ROWS)
    small = dot(act, misc[:, 0:256])
    kv = small[:, 0:128].astype(bf16)
    logits = jnp.where(lane < E, small[:, 128:256], masked_value)
    top = jnp.max(logits, -1, keepdims=True)
    lane_f = lane.astype(f32)
    hit = [hc[:, k : k + 1] == lane_f for k in range(TOPK)]
    chosen = hit[0]
    for k in range(1, TOPK):
        chosen = chosen | hit[k]
    powers = jnp.where(chosen, jnp.exp(logits - top), 0.0)
    gate = powers / jnp.sum(powers, -1, keepdims=True)
    gate_ref[...] = gate
    gate_low = gate.astype(bf16).astype(f32)
    gates = [jnp.sum(jnp.where(hit[k], gate_low, 0.0), -1, keepdims=True) for k in range(TOPK)]
    compact = jnp.zeros((ROWS, 128), f32)
    for p in range(PAIRS):
        compact = jnp.where(lane == p, gates[2 * p], compact)
        compact = jnp.where(lane == 64 + p, gates[2 * p + 1], compact)
    gsl_ref[...] = compact
    kv_ref[...] = kv
    row = pl.multiple_of(step * ROWS, ROWS)
    kv_f = kv.astype(f32)
    k_lo = jnp.where(low_half, kv_f, 0.0)
    k_hi = pltpu.roll(k_lo, 64, 1)
    val_hi = jnp.where(low_half, 0.0, kv_f)
    val_lo = pltpu.roll(val_hi, 64, 1)
    kt_lo[:, pl.ds(row, ROWS)] = k_lo.T.astype(bf16)
    kt_hi[:, pl.ds(row, ROWS)] = k_hi.T.astype(bf16)
    ones = jnp.where(low_half, 1.0, 0.0)
    v_lo[pl.ds(row, ROWS), 0:128] = val_lo.astype(bf16)
    v_lo[pl.ds(row, ROWS), 128:256] = ones.astype(bf16)
    v_hi[pl.ds(row, ROWS), 0:128] = val_hi.astype(bf16)
    v_hi[pl.ds(row, ROWS), 128:256] = (1.0 - ones).astype(bf16)
    queries = dot(act, wq[...])
    picked = pick_heads(queries, slots)
    for p in range(PAIRS):
        scaled = picked[p] * jnp.asarray(H ** (-0.5), bf16)
        qs_ref[:, p * 128 : (p + 1) * 128] = scaled
        for s in range(ROWS // SUB):
            qst[s, p * SUB : (p + 1) * SUB, :] = scaled[s * SUB : (s + 1) * SUB]

    for s in range(ROWS // SUB):
        block = step * (ROWS // SUB) + s
        count = idx[VDP + VTP + block]
        rows = slice(s * SUB, (s + 1) * SUB)

        def attend(n, s=s, block=block, rows=rows):
            width = n * SUB
            start = pl.multiple_of((block + 1 - n) * SUB, SUB)
            bias = bias_of(segc_ref[rows, :], segr_ref, block * SUB, start, width)
            q4 = qst[s]
            parts = []
            tops = []
            for kt in (kt_lo, kt_hi):
                scores = dot(q4, kt[:, pl.ds(start, width)]).reshape(PAIRS, SUB, width) + bias[None]
                peak = jnp.max(scores, -1, keepdims=True)
                parts.append(jnp.exp(scores - peak).astype(bf16).reshape(PAIRS * SUB, width))
                tops.append(peak.reshape(PAIRS * SUB, 1))
            result = dot(parts[0], v_lo[pl.ds(start, width), :]) + dot(parts[1], v_hi[pl.ds(start, width), :])
            total = result[:, 128:256]
            heads = result[:, 0:128] / total
            log_sum = jnp.where(lanes(PAIRS * SUB) < 64, tops[0], tops[1]) + jnp.log(total)
            keep = jnp.zeros((SUB, 128), f32)
            for p in range(PAIRS):
                one = slice(p * SUB, (p + 1) * SUB)
                ho_ref[rows, p * 128 : (p + 1) * 128] = heads[one]
                keep = jnp.where((lanes(SUB) & 63) == p, log_sum[one], keep)
            lse_ref[rows, :] = keep

        for n in range(1, 6):
            pl.when(count == n)(functools.partial(attend, n))

    mixed = []
    for p in range(PAIRS):
        gate_pair = jnp.where(low_half, gates[2 * p], gates[2 * p + 1])
        mixed.append(gate_pair * ho_ref[:, p * 128 : (p + 1) * 128])

    def store(c, value):
        spread_ref[:, c * 128 : (c + 1) * 128] = value

    spread_heads(mixed, slots, store)
    mid_ref[...] = x + dot_nt(spread_ref[...], wo[...])


def ffn_forward_kernel(last, idx, x_ref, gains_ref, *rest):
    w_refs = rest[:VDP]
    out_ref = rest[VDP]
    wu, wd = rest[VDP + 1 :]

    @pl.when(pl.program_id(0) == 0)
    def _():
        place(w_refs, wu, idx, 0, RW, CF)
        place(w_refs, wd, idx, RW, RW, CF)

    x = x_ref[...]
    normed, _ = normalize(x)
    act = (normed * gains_ref[1:2, :]).astype(bf16)
    pre = dot(act, wu[...])
    hidden = jax.nn.gelu(pre, approximate=True).astype(bf16)
    out_ref[...] = (x + dot_nt(hidden, wd[...])).astype(out_ref.dtype)


def ffn_backward_kernel(idx, up_ref, x_ref, gains_ref, *rest):
    w_refs = rest[:VDP]
    mid_ref, gain_ref, keep_ref, send_ref = rest[VDP : VDP + 4]
    wu, wd, hid_s, gp_s, grad_t, act_t, part = rest[VDP + 4 :]
    step = pl.program_id(0)

    @pl.when(step == 0)
    def _():
        place(w_refs, wu, idx, 0, RW, CF)
        place(w_refs, wd, idx, RW, RW, CF)
        gain_ref[...] = jnp.zeros_like(gain_ref)

    @pl.when(step < STEPS)
    def _():
        row = pl.multiple_of(step * ROWS, ROWS)
        up = up_ref[...].astype(f32)
        gain = gains_ref[1:2, :]
        normed, factor = normalize(x_ref[...])
        act_f = normed * gain
        act = act_f.astype(bf16)
        act_t[:, pl.ds(row, ROWS)] = act_f.T.astype(bf16)
        grad_t[:, pl.ds(row, ROWS)] = up.T.astype(bf16)
        pre = dot(act, wu[...])
        grad_hidden = dot(up.astype(bf16), wd[...])
        square = pre * pre
        arg = 0.7978845608028654 * pre * (1.0 + 0.044715 * square)
        bend = jnp.tanh(arg)
        half = 0.5 * (1.0 + bend)
        hid_s[pl.ds(row, ROWS), :] = (pre * half).astype(bf16)
        slope = half + (0.5 * 0.7978845608028654) * pre * (1.0 - bend * bend) * (
            1.0 + 3.0 * 0.044715 * square
        )
        grad_pre = (grad_hidden * slope).astype(bf16)
        gp_s[pl.ds(row, ROWS), :] = grad_pre
        grad_act = dot_nt(grad_pre, wu[...])
        scaled = grad_act * gain
        inner = jnp.mean(scaled * normed, -1, keepdims=True)
        mid_ref[...] = up + factor * (scaled - normed * inner)
        gain_ref[0:1, :] += jnp.sum(grad_act * normed, 0, keepdims=True)

    @pl.when(step >= STEPS)
    def _():
        q = step - STEPS
        col = pl.multiple_of(idx[VDP + q] * CF, CF)
        part[...] = dot(act_t[...], gp_s[:, pl.ds(col, CF)])
        hand_out(keep_ref, send_ref, part, idx, 0, RW)
        part[...] = dot(grad_t[...], hid_s[:, pl.ds(col, CF)])
        hand_out(keep_ref, send_ref, part, idx, RW, RW)


def output_backward_kernel(idx, mid_ref, hc_ref, ho_ref, gate_ref, gsl_ref, spread_ref, *rest):
    w_refs = rest[:VDP]
    gh_ref, dd_ref, gl_ref, keep_ref, send_ref = rest[VDP : VDP + 5]
    wo, grad_t, part = rest[VDP + 5 :]
    step = pl.program_id(0)

    @pl.when(step == 0)
    def _():
        place(w_refs, wo, idx, RW, RW, CA)

    @pl.when(step < STEPS)
    def _():
        row = pl.multiple_of(step * ROWS, ROWS)
        mid = mid_ref[...]
        grad_t[:, pl.ds(row, ROWS)] = mid.T.astype(bf16)
        full = dot(mid.astype(bf16), wo[...])
        hc = hc_ref[...]
        slots = slot_columns(hc)
        mixed = pick_heads(full, slots)
        lane = lanes(ROWS)
        low_half = lane < 64
        lane_f = lane.astype(f32)
        gsl = gsl_ref[...]
        inner = jnp.zeros((ROWS, 128), f32)
        grad_gates = jnp.zeros((ROWS, 128), f32)
        for p in range(PAIRS):
            value = mixed[p].astype(f32)
            ga = gsl[:, p : p + 1]
            gb = gsl[:, 64 + p : 65 + p]
            gh_ref[:, p * 128 : (p + 1) * 128] = (jnp.where(low_half, ga, gb) * value).astype(bf16)
            product = value * ho_ref[:, p * 128 : (p + 1) * 128]
            sum_a = jnp.sum(jnp.where(low_half, product, 0.0), -1, keepdims=True)
            sum_b = jnp.sum(jnp.where(low_half, 0.0, product), -1, keepdims=True)
            inner = jnp.where(lane == p, ga * sum_a, inner)
            inner = jnp.where(lane == 64 + p, gb * sum_b, inner)
            grad_gates = jnp.where(hc[:, 2 * p : 2 * p + 1] == lane_f, sum_a, grad_gates)
            grad_gates = jnp.where(hc[:, 2 * p + 1 : 2 * p + 2] == lane_f, sum_b, grad_gates)
        dd_ref[...] = inner
        gate = gate_ref[...]
        total = jnp.sum(gate * grad_gates, -1, keepdims=True)
        gl_ref[...] = (gate * (grad_gates - total)).astype(bf16)

    @pl.when(step >= STEPS)
    def _():
        q = step - STEPS
        col = pl.multiple_of(idx[VDP + q] * CA, 128)
        part[...] = dot(grad_t[...], spread_ref[:, pl.ds(col, CA)])
        hand_out(keep_ref, send_ref, part, idx, 0, RW)


def attn_backward_kernel(
    idx, mid_ref, x_ref, hc_ref, segc_ref, segr_ref, qs_ref, gh_ref, kv_ref, lse_ref, dd_ref, gl_ref, gains_ref, gfg_ref, *rest
):
    w_refs = rest[:VDP]
    out_ref, keep_ref, send_ref = rest[VDP : VDP + 3]
    (wq, misc, kt_lo, kt_hi, vt_lo, vt_hi, k_lo, k_hi, dkv_t, qst, gst, dq_s, gq_s, act_t, dkv_s, gain_s, part, pmisc) = rest[
        VDP + 3 :
    ]
    step = pl.program_id(0)

    @pl.when(step == 0)
    def _():
        place(w_refs, wq, idx, 0, RW, CA)
        place_misc(w_refs, misc, idx, 2 * RW)
        low = lanes(LEN) < 64
        kv = kv_ref[...].astype(f32)
        one = jnp.where(low, kv, 0.0)
        two = pltpu.roll(one, 64, 1)
        k_lo[...] = one.astype(bf16)
        k_hi[...] = two.astype(bf16)
        kt_lo[...] = one.T.astype(bf16)
        kt_hi[...] = two.T.astype(bf16)
        one = jnp.where(low, 0.0, kv)
        vt_hi[...] = one.T.astype(bf16)
        vt_lo[...] = pltpu.roll(one, 64, 1).T.astype(bf16)
        dkv_t[...] = jnp.zeros_like(dkv_t)
        gain_s[...] = jnp.zeros_like(gain_s)

    @pl.when(step < STEPS)
    def _():
        row = pl.multiple_of(step * ROWS, ROWS)
        for p in range(PAIRS):
            for s in range(ROWS // SUB):
                qst[s, p * SUB : (p + 1) * SUB, :] = qs_ref[s * SUB : (s + 1) * SUB, p * 128 : (p + 1) * 128]
                gst[s, p * SUB : (p + 1) * SUB, :] = gh_ref[s * SUB : (s + 1) * SUB, p * 128 : (p + 1) * 128]
        for s in range(ROWS // SUB):
            block = step * (ROWS // SUB) + s
            count = idx[VDP + VTP + block]
            rows = slice(s * SUB, (s + 1) * SUB)

            def attend(n, s=s, block=block, rows=rows):
                width = n * SUB
                start = pl.multiple_of((block + 1 - n) * SUB, SUB)
                win = pl.ds(start, width)
                bias = bias_of(segc_ref[rows, :], segr_ref, block * SUB, start, width)
                q4 = qst[s]
                g4 = gst[s]
                q4t = q4.astype(f32).T.astype(bf16)
                g4t = g4.astype(f32).T.astype(bf16)
                lse = lse_ref[rows, :]
                dd = dd_ref[rows, :]
                dq = None
                dk = None
                dv = None
                for half, (kt, vt, kk) in enumerate(((kt_lo, vt_lo, k_lo), (kt_hi, vt_hi, k_hi))):
                    off = 64 * half
                    log_sum = jnp.stack([lse[:, off + p : off + p + 1] for p in range(PAIRS)])
                    inner = jnp.stack([dd[:, off + p : off + p + 1] for p in range(PAIRS)])
                    scores = dot(q4, kt[:, win]).reshape(PAIRS, SUB, width)
                    prob = jnp.exp(scores + bias[None] - log_sum)
                    dprob = dot(g4, vt[:, win]).reshape(PAIRS, SUB, width)
                    dscore = (prob * (dprob - inner)).astype(bf16).reshape(PAIRS * SUB, width)
                    low_prob = prob.astype(bf16).reshape(PAIRS * SUB, width)
                    a = dot(dscore, kk[win, :])
                    b = dot(q4t[off : off + 64], dscore)
                    c = dot(g4t[off : off + 64], low_prob)
                    dq = a if dq is None else dq + a
                    dk = b if dk is None else dk + b
                    dv = c if dv is None else dv + c
                dkv_t[0:64, win] += dk
                dkv_t[64:128, win] += dv
                dq = dq * (H ** (-0.5))
                for p in range(PAIRS):
                    dq_s[rows, p * 128 : (p + 1) * 128] = dq[p * SUB : (p + 1) * SUB]

            for n in range(1, 6):
                pl.when(count == n)(functools.partial(attend, n))

        slots = slot_columns(hc_ref[...])

        def store(c, value):
            gq_s[pl.ds(row, ROWS), c * 128 : (c + 1) * 128] = value

        spread_heads([dq_s[:, p * 128 : (p + 1) * 128] for p in range(PAIRS)], slots, store)

    @pl.when(step == STEPS)
    def _():
        dkv_s[...] = dkv_t[...].T.astype(bf16)

    @pl.when((step >= STEPS) & (step < 2 * STEPS))
    def _():
        row = pl.multiple_of((step - STEPS) * ROWS, ROWS)
        here = pl.ds(row, ROWS)
        gain = gains_ref[0:1, :]
        normed, factor = normalize(x_ref[...].astype(f32))
        act_t[:, here] = (normed * gain).T.astype(bf16)
        grad_act = dot_nt(gq_s[here, :], wq[...])
        grad_act += dot_nt(dkv_s[here, :], misc[:, 0:128])
        router = jnp.where(lanes(D) < E, misc[:, 128:256].astype(f32), 0.0).astype(bf16)
        grad_act += dot_nt(gl_ref[here, :], router)
        scaled = grad_act * gain
        inner = jnp.mean(scaled * normed, -1, keepdims=True)
        out_ref[...] = mid_ref[...] + factor * (scaled - normed * inner)
        gain_s[0:1, :] += jnp.sum(grad_act * normed, 0, keepdims=True)

    @pl.when(step == 2 * STEPS)
    def _():
        pmisc[:, 0:128] = dot(act_t[...], dkv_s[...])
        router = dot(act_t[...], gl_ref[...])
        gain_s[1:2, :] = gfg_ref[0:1, :]
        turned = gain_s[...].T
        lane = lanes(D)
        router = jnp.where(lane < E, router, 0.0)
        router = jnp.where(lane == E, turned[:, 0:1], router)
        router = jnp.where(lane == E + 1, turned[:, 1:2], router)
        pmisc[:, 128:256] = router
        pmisc[:, 256:384] = jnp.zeros((D, 128), f32)

    @pl.when(step >= 2 * STEPS)
    def _():
        q = step - 2 * STEPS
        col = pl.multiple_of(idx[VDP + q] * CA, 128)
        part[...] = dot(act_t[...], gq_s[:, pl.ds(col, CA)])
        hand_out(keep_ref, send_ref, part, idx, 0, RW)
        for j in range(VDP):
            row = pl.multiple_of((idx[j] * VTP + idx[VDP + q]) * RM, RM)
            target = keep_ref if j % 2 == 0 else send_ref
            target[j // 2, 0, RW : RW + RM, :] = pmisc[pl.ds(row, RM), :].astype(bf16)


def rows_spec(width, phase=0, single=False):
    def index(i, idx):
        return (jnp.clip(i - phase * STEPS, 0, STEPS - 1), 0)

    return pl.BlockSpec((ROWS, width), index)


def full_spec(shape):
    zeros = (0,) * len(shape)
    return pl.BlockSpec(shape, lambda i, idx: zeros, pipeline_mode=pl.Buffered(1))


def kept_spec(shape):
    zeros = (0,) * len(shape)
    return pl.BlockSpec(shape, lambda i, idx: zeros)


def parts_spec(rows, width, phase):
    def index(i, idx):
        return (0, jnp.maximum(i - phase * STEPS, 0), 0, 0)

    return pl.BlockSpec((4, 1, rows, width), index)


def call(kernel, steps, in_specs, out_specs, out_shapes, scratch, name, flops, moved):
    return pl.pallas_call(
        kernel,
        grid_spec=pltpu.PrefetchScalarGridSpec(
            num_scalar_prefetch=1,
            grid=(steps,),
            in_specs=in_specs,
            out_specs=out_specs,
            scratch_shapes=scratch,
        ),
        out_shape=[jax.ShapeDtypeStruct(s, d) for s, d in out_shapes],
        compiler_params=pltpu.CompilerParams(
            dimension_semantics=("arbitrary",), vmem_limit_bytes=VMEM
        ),
        cost_estimate=pl.CostEstimate(flops=flops, bytes_accessed=moved, transcendentals=0),
        name=name,
    )


def vm(*shape, dtype=bf16):
    return pltpu.VMEM(shape, dtype)


def attn_forward(idx, x, hc, segc, segr, weights):
    return call(
        attn_forward_kernel,
        STEPS,
        [rows_spec(D), rows_spec(TOPK), rows_spec(128), full_spec((8, LEN))]
        + [full_spec((VTP * RA, CA))] * VDP,
        [
            rows_spec(D), rows_spec(KH), rows_spec(128), rows_spec(KH), rows_spec(128),
            rows_spec(EH), rows_spec(128), rows_spec(128), kept_spec((8, D)),
        ],
        [
            ((LEN, D), f32), ((LEN, KH), bf16), ((LEN, 128), bf16), ((LEN, KH), f32), ((LEN, 128), f32),
            ((LEN, EH), bf16), ((LEN, 128), f32), ((LEN, 128), f32), ((8, D), f32),
        ],
        [
            vm(D, EH), vm(D, EH), vm(D, 384), vm(8, D, dtype=f32), vm(128, LEN), vm(128, LEN),
            vm(LEN, 256), vm(LEN, 256), vm(ROWS // SUB, PAIRS * SUB, 128), vm(ROWS, 128),
        ],
        "attn_forward", 8 * 10**9, 14 * 10**6,
    )(idx, x, hc, segc, segr, *weights)


def ffn_forward(idx, x, gains, weights, last):
    return call(
        functools.partial(ffn_forward_kernel, last),
        STEPS,
        [rows_spec(D), full_spec((8, D))] + [full_spec((VTP * 2 * RW, CF))] * VDP,
        [rows_spec(D)],
        [((LEN, D), bf16 if last else f32)],
        [vm(D, FF), vm(D, FF)],
        "ffn_forward", 5 * 10**9, 8 * 10**6,
    )(idx, x, gains, *weights)[0]


def ffn_backward(idx, upstream, x, gains, weights):
    return call(
        ffn_backward_kernel,
        2 * STEPS,
        [rows_spec(D), rows_spec(D), full_spec((8, D))] + [full_spec((VTP * 2 * RW, CF))] * VDP,
        [rows_spec(D), kept_spec((8, D)), parts_spec(2 * RW, CF, 1), parts_spec(2 * RW, CF, 1)],
        [
            ((LEN, D), f32), ((8, D), f32),
            ((4, VTP, 2 * RW, CF), bf16), ((4, VTP, 2 * RW, CF), bf16),
        ],
        [
            vm(D, FF), vm(D, FF), vm(LEN, FF), vm(LEN, FF), vm(D, LEN), vm(D, LEN), vm(D, CF, dtype=f32),
        ],
        "ffn_backward", 13 * 10**9, 14 * 10**6,
    )(idx, upstream, x, gains, *weights)


def output_backward(idx, mid, hc, heads, gate, gsl, spread, weights):
    return call(
        output_backward_kernel,
        2 * STEPS,
        [rows_spec(D), rows_spec(TOPK), rows_spec(KH), rows_spec(128), rows_spec(128), full_spec((LEN, EH))]
        + [full_spec((VTP * RA, CA))] * VDP,
        [rows_spec(KH), rows_spec(128), rows_spec(128), parts_spec(RW, CA, 1), parts_spec(RW, CA, 1)],
        [
            ((LEN, KH), bf16), ((LEN, 128), f32), ((LEN, 128), bf16),
            ((4, VTP, RW, CA), bf16), ((4, VTP, RW, CA), bf16),
        ],
        [vm(D, EH), vm(D, LEN), vm(D, CA, dtype=f32)],
        "output_backward", 5 * 10**9, 16 * 10**6,
    )(idx, mid, hc, heads, gate, gsl, spread, *weights)


def attn_backward(idx, mid, x, hc, segc, segr, qs, gh, kv, lse, dd, gl, gains, gfg, weights):
    return call(
        attn_backward_kernel,
        3 * STEPS,
        [
            rows_spec(D, 1), rows_spec(D, 1), rows_spec(TOPK), rows_spec(128), full_spec((8, LEN)),
            rows_spec(KH), rows_spec(KH), full_spec((LEN, 128)), rows_spec(128), rows_spec(128),
            full_spec((LEN, 128)), full_spec((8, D)), full_spec((8, D)),
        ]
        + [full_spec((VTP * RA, CA))] * VDP,
        [rows_spec(D, 1), parts_spec(RQ, CA, 2), parts_spec(RQ, CA, 2)],
        [((LEN, D), f32), ((4, VTP, RQ, CA), bf16), ((4, VTP, RQ, CA), bf16)],
        [
            vm(D, EH), vm(D, 384), vm(128, LEN), vm(128, LEN), vm(128, LEN), vm(128, LEN),
            vm(LEN, 128), vm(LEN, 128), vm(128, LEN, dtype=f32), vm(ROWS // SUB, PAIRS * SUB, 128),
            vm(ROWS // SUB, PAIRS * SUB, 128), vm(ROWS, KH, dtype=f32), vm(LEN, EH), vm(D, LEN),
            vm(LEN, 128), vm(8, D, dtype=f32), vm(D, CA, dtype=f32), vm(D, 384, dtype=f32),
        ],
        "attn_backward", 10 * 10**9, 16 * 10**6,
    )(idx, mid, x, hc, segc, segr, qs, gh, kv, lse, dd, gl, gains, gfg, *weights)


def shift(size, k):
    return [(i, (i - k) % size) for i in range(size)]


def unshift(size, k):
    return [(i, (i + k) % size) for i in range(size)]


def swap(k):
    return [(i, i ^ k) for i in range(VDP)]


def gather_piece(mine):
    stack = jnp.concatenate(
        [mine] + [lax.ppermute(mine, "tp", unshift(VTP, k)) for k in range(1, VTP)], 0
    )
    plane = [stack] + [lax.ppermute(stack, "dp", swap(2 * k)) for k in range(1, 4)]
    other = [lax.ppermute(part, "dp", swap(1)) for part in plane]
    return [plane[j // 2] if j % 2 == 0 else other[j // 2] for j in range(VDP)]


def reduce_piece(keep, send):
    got = lax.ppermute(send, "dp", swap(1))
    pair = [(keep[k].astype(f32) + got[k].astype(f32)).astype(bf16) for k in range(4)]
    total = pair[0].astype(f32)
    for k in range(1, 4):
        total = total + lax.ppermute(pair[k], "dp", swap(2 * k)).astype(f32)
    line = total.astype(bf16)
    total = line[0].astype(f32)
    for k in range(1, VTP):
        total = total + lax.ppermute(line[k], "tp", shift(VTP, k)).astype(f32)
    return total


def block_piece(whole_parts, misc):
    out = []
    for j in range(VDP):
        stack = []
        for q in range(VTP):
            for part in whole_parts:
                width = part.shape[1] // VTP
                stack.append(part[j * RW : (j + 1) * RW, q * width : (q + 1) * width])
            if misc is not None:
                row = (j * VTP + q) * RM
                stack.append(misc[row : row + RM])
        out.append(jnp.concatenate(stack, 0))
    return out


def unblock_piece(keep, send, counts):
    both = jnp.stack([keep, send], 1).reshape((VDP,) + keep.shape[1:])
    out = []
    first = 0
    for count in counts:
        part = both[:, :, first : first + count]
        first += count
        if count == RW:
            out.append(part.transpose(0, 2, 1, 3).reshape(D, VTP * part.shape[3]))
        else:
            out.append(part.reshape(D, part.shape[3]))
    return out


def split_gain(gain):
    high = lax.reduce_precision(gain, 8, 7)
    rest = gain - high
    middle = lax.reduce_precision(rest, 8, 7)
    return [high, middle, rest - middle]


def global_sum(value, native):
    if not native:
        return lax.psum(value, ("dp", "tp"))
    total = value
    for k in range(1, VDP):
        total = total + lax.ppermute(value, "dp", swap(k))
    out = total
    for k in range(1, VTP):
        out = out + lax.ppermute(total, "tp", shift(VTP, k))
    return out


def adamw(weight, moment_one, moment_two, average, grad_full, factor, learn_rate):
    clipped = grad_full * factor
    first_new = beta_one * moment_one + (1.0 - beta_one) * clipped
    second_new = beta_two * moment_two + (1.0 - beta_two) * clipped * clipped
    step_ratio = (
        first_new
        / (1.0 - beta_one**STEP)
        / (jnp.sqrt(second_new / (1.0 - beta_two**STEP)) + adam_floor)
    )
    weight_new = weight - learn_rate * (step_ratio + weight_decay * weight)
    return (weight_new, first_new, second_new, ema_decay * average + (1.0 - ema_decay) * weight_new)


def local(tokens, cotangent, head_choice, segment_ids, *state):
    weights, firsts, seconds, averages = state[0:7], state[7:14], state[14:21], state[21:28]
    query_w, output_w, up_w, down_w, keyval_w, router_w, gains_w = weights
    size_dp = lax.axis_size("dp")
    size_tp = lax.axis_size("tp")
    token_total = tokens.shape[0] * size_dp * size_tp
    native = (size_dp, size_tp) == (VDP, VTP)
    gain_parts = split_gain(gains_w)
    low_parts = [w.astype(bf16) for w in weights[:6]]

    def small_rows(l, kv, router, gains):
        columns = [g[l, which].astype(bf16)[:, None] for which in range(2) for g in gains]
        block = jnp.concatenate([kv[l], router[l]] + columns, 1)
        return jnp.pad(block, ((0, 0), (0, CA - block.shape[1])))

    pieces_a, pieces_f = [], []
    if native:
        own = jnp.arange(VDP, dtype=jnp.int32) ^ lax.axis_index("dp").astype(jnp.int32)
        line = (lax.axis_index("tp").astype(jnp.int32) - jnp.arange(VTP, dtype=jnp.int32)) % VTP
        for l in range(LAYERS):
            misc = small_rows(l, low_parts[4], low_parts[5], gain_parts)
            pieces_a.append(gather_piece(jnp.concatenate([low_parts[0][l], low_parts[1][l], misc], 0)))
            pieces_f.append(gather_piece(jnp.concatenate([low_parts[2][l], low_parts[3][l]], 0)))
    else:
        own = jnp.arange(VDP, dtype=jnp.int32)
        line = jnp.arange(VTP, dtype=jnp.int32)
        big = [
            lax.all_gather(lax.all_gather(w, "dp", axis=1, tiled=True), "tp", axis=2, tiled=True)
            for w in low_parts[:4]
        ]
        small = [lax.all_gather(w, ("dp", "tp"), axis=1, tiled=True) for w in low_parts[4:6]]
        wide = [lax.all_gather(g, ("dp", "tp"), axis=2, tiled=True) for g in gain_parts]
        for l in range(LAYERS):
            misc = small_rows(l, small[0], small[1], wide)
            pieces_a.append(block_piece([big[0][l], big[1][l]], misc))
            pieces_f.append(block_piece([big[2][l], big[3][l]], None))

    segment = segment_ids.reshape(LEN)
    heads_at = segment[:: SUB]
    first_at = jnp.sum((segment[None, :] < heads_at[:, None]).astype(jnp.int32), 1)
    blocks = jnp.arange(LEN // SUB, dtype=jnp.int32) - first_at // SUB + 1
    idx = jnp.concatenate([own, line, blocks])
    segc = jnp.broadcast_to(segment.astype(f32)[:, None], (LEN, 128))
    segr = jnp.broadcast_to(segment.astype(f32)[None, :], (8, LEN))
    hc = head_choice.astype(f32)

    saved = []
    residual = tokens
    for l in range(LAYERS):
        mid, qs, kv, heads, lse, spread, gate, gsl, gains = attn_forward(
            idx, residual, hc, segc, segr, pieces_a[l]
        )
        saved.append((residual, mid, qs, kv, heads, lse, spread, gate, gsl, gains))
        residual = ffn_forward(idx, mid, gains, pieces_f[l], l == LAYERS - 1)
    layer_out = residual

    upstream = cotangent
    parts = [None] * LAYERS
    for l in reversed(range(LAYERS)):
        residual, mid, qs, kv, heads, lse, spread, gate, gsl, gains = saved[l]
        mid_grad, gain_ffn_grad, keep_f, send_f = ffn_backward(idx, upstream, mid, gains, pieces_f[l])
        gh, dd, gl, keep_o, send_o = output_backward(
            idx, mid_grad, hc, heads, gate, gsl, spread, pieces_a[l]
        )
        upstream, keep_q, send_q = attn_backward(
            idx, mid_grad, residual, hc, segc, segr, qs, gh, kv, lse, dd, gl, gains, gain_ffn_grad, pieces_a[l]
        )
        parts[l] = ((keep_q, send_q), (keep_o, send_o), (keep_f, send_f))

    scale = 1.0 / token_total
    if native:
        done = [[reduce_piece(*piece) for piece in parts[l]] for l in range(LAYERS)]
        sums = [
            jnp.stack([d[0][:RW] for d in done]),
            jnp.stack([d[1] for d in done]),
            jnp.stack([d[2][:RW] for d in done]),
            jnp.stack([d[2][RW:] for d in done]),
            jnp.stack([d[0][RW:, :128] for d in done]),
            jnp.stack([d[0][RW:, 128 : 128 + E] for d in done]),
            jnp.stack([d[0][RW:, 128 + E : 130 + E].T for d in done]),
        ]
    else:
        whole = []
        for l in range(LAYERS):
            grad_q, misc = unblock_piece(*parts[l][0], (RW, RM))
            (grad_o,) = unblock_piece(*parts[l][1], (RW,))
            grad_u, grad_d = unblock_piece(*parts[l][2], (RW, RW))
            whole.append((grad_q, grad_o, grad_u, grad_d, misc))
        sums = []
        for i in range(4):
            grad = jnp.stack([w[i] for w in whole]).astype(f32)
            grad = lax.psum_scatter(grad, "tp", scatter_dimension=2, tiled=True)
            sums.append(lax.psum_scatter(grad, "dp", scatter_dimension=1, tiled=True))
        misc = jnp.stack([w[4] for w in whole]).astype(f32)
        misc = lax.psum_scatter(misc, ("dp", "tp"), scatter_dimension=1, tiled=True)
        sums += [misc[:, :, :128], misc[:, :, 128 : 128 + E], misc[:, :, 128 + E : 130 + E].transpose(0, 2, 1)]
    sums = [s * scale for s in sums]
    squares = jnp.sum(jnp.stack([jnp.sum(s * s) for s in sums]))
    grad_norm = jnp.sqrt(global_sum(squares.reshape(1, 1), native))[0, 0]
    factor = jnp.minimum(1.0, clip_bound / grad_norm)
    outs = [layer_out, upstream, grad_norm]
    for i in range(7):
        outs += adamw(weights[i], firsts[i], seconds[i], averages[i], sums[i], factor, learn_rates[i])
    return tuple(outs)


def solution(mesh):
    token = P(("dp", "tp"), None)
    big = P(None, "dp", "tp")
    small = P(None, ("dp", "tp"), None)
    gain = P(None, None, ("dp", "tp"))
    group = (big, big, big, big, small, small, gain)
    in_specs = (token,) * 4 + group * 4
    out_specs = (token, token, P()) + tuple(spec for spec in group for _ in range(4))
    return jax.shard_map(local, mesh=mesh, in_specs=in_specs, out_specs=out_specs, check_vma=False)
```

time: 3010 us -> 507 us (0.17)
  waiting for transfers between devices: 1470 us -> 133 us
  local copies, waits for them, and re-layouts: 720 us -> 12 us
  matrix products: 345 us -> 0 us
  blocking collectives: 275 us -> 0 us
  Pallas kernels: 0 us -> 203 us
  other arithmetic: 165 us -> 30.8 us
  starting transfers between devices: 0.87 us -> 109 us
    reduce_scatter x11 -> x0, waiting for transfers between devices: 880 us -> none  [the longest x2 286 us: local(): ffn_out = lax.psum_scatter(ffn_out, 'tp', scatter_dimension=0, tiled=True)]
    gather x18 -> x0, local copies, waits for them, and re-layouts: 587 us -> none  [the longest x4 246 us: local(): grad_mixed = jnp.take_along_axis(grad_spread, slot_index, axis=1)]
    dot_general x64 -> x0, matrix products: 345 us -> none  [the longest x24 94.6 us: contract(): lax.dot_general(left_op, right_op, (((left_dim,), (right_dim,)), ((), ())...]
    all_gather x8 -> x0, waiting for transfers between devices: 329 us -> none  [the longest x2 158 us: local(): group_ffn = lax.all_gather(act_ffn, 'tp', axis=0, tiled=True)]
    unnamed x23 -> x0, waiting for transfers between devices: 261 us -> none
    all_gather x5 -> x0, blocking collectives: 235 us -> none  [the longest x1 73.3 us: local(): lax.all_gather(router_weight, ('dp', 'tp'), axis=1, tiled=True)]
    pallas_call x0 -> x10, Pallas kernels: none -> 203 us  [the longest x2 57.3 us: attn_backward(): call(attn_backward_kernel, 3 * STEPS, [rows_spec(D, 1), rows_spec(D, 1),...]
    ppermute x0 -> x92, waiting for transfers between devices: none -> 133 us  [the longest x18 49.3 us: reduce_piece(): total = total + lax.ppermute(pair[k], 'dp', swap(2 * k)).astype(f32)]
  transfers between devices with their start and end apart: 21 -> 92, of which waited for: 17 -> 38; matrix products, arithmetic and copies ran while one was open for 21% -> 6% of each run, Pallas kernels for 0% -> 19%
where the time goes in v1:
time: 507 us; the launch traced here: 503 us
  Pallas kernels  203 us (40%)
  waiting for transfers between devices  133 us (26%)
  starting transfers between devices  109 us (21%)
  other arithmetic  30.8 us (6%)
  between operations  13.9 us (3%)
  local copies, waits for them, and re-layouts  12 us (2%)
    pallas_call x2, Pallas kernels, attn_backward(): call(attn_backward_kernel, 3 * STEPS, [rows_spec(D, 1), rows_spec(D, 1),...  57.3 us
    ppermute x18, waiting for transfers between devices, reduce_piece(): total = total + lax.ppermute(pair[k], 'dp', swap(2 * k)).astype(f32)  49.3 us
    pallas_call x2, Pallas kernels, attn_forward(): call(attn_forward_kernel, STEPS, [rows_spec(D), rows_spec(TOPK), rows_spe...  47 us
    ppermute x12, waiting for transfers between devices, gather_piece(): lax.ppermute(stack, 'dp', swap(2 * k))  41.9 us
    pallas_call x2, Pallas kernels, ffn_backward(): call(ffn_backward_kernel, 2 * STEPS, [rows_spec(D), rows_spec(D), full_sp...  41.6 us
    pallas_call x2, Pallas kernels, output_backward(): call(output_backward_kernel, 2 * STEPS, [rows_spec(D), rows_spec(TOPK), r...  35.9 us
    ppermute x12, waiting for transfers between devices, gather_piece(): lax.ppermute(mine, 'tp', unshift(VTP, k))  24.1 us
    ppermute x18, starting transfers between devices, reduce_piece(): total = total + lax.ppermute(pair[k], 'dp', swap(2 * k)).astype(f32)  23.6 us
  transfers between devices with their start and end apart: 92, of which 38 were waited for; matrix products, arithmetic and copies ran while one was open for 6% of the time, Pallas kernels for 19%

profile of v1, /device:TPU:0, one launch (start us, length us, event | category | flops | bytes accessed | tf_op | source)
XLA Modules:
  0.0 502.7 jit_solution(7279366073083483821)
XLA Ops:
  2.7 5.1 %collective-permute-start.12 = (bf16[128,512]{1,0:T(8,128)(2,1)S(1)}, bf16[128,512]{1,0:T(8,128)(2,1)S(1)}, u32[]{:S(2)}, u32[]{:S(2)}) collective-permute-start(bf16[128,512]{1,0:T(8,128)(2,1)S(1)} %pad_maximum_fusion.4), channel_id=1, source_target_pairs={{0,3},{1,0},{2,1},{3,2},{4,7},{5,4},{6,5},{7,6},{8,11},{9,8},{10,9... | collective-permute-start | bytes 393224 | tf_op jit(solution)/shard_map/ppermute | solution.py:646
  18.5 6.4 %collective-permute-done = bf16[144,384]{1,0:T(8,128)(2,1)S(1)} collective-permute-done((bf16[144,384]{1,0:T(8,128)(2,1)S(1)}, bf16[144,384]{1,0:T(8,128)(2,1)S(1)}, u32[]{:S(2)}, u32[]{:S(2)}) %collective-permute-start) | collective-permute-done | bytes 110624 | tf_op jit(solution)/shard_map/ppermute | solution.py:646
  26.6 4.9 collective-permute-done.1
  45.3 5.3 %collective-permute-done.21 = bf16[144,384]{1,0:T(8,128)(2,1)S(1)} collective-permute-done((bf16[144,384]{1,0:T(8,128)(2,1)S(1)}, bf16[144,384]{1,0:T(8,128)(2,1)S(1)}, u32[]{:S(2)}, u32[]{:S(2)}) %collective-permute-start.21) | collective-permute-done | bytes 110624 | tf_op jit(solution)/shard_map/ppermute | solution.py:646
  70.5 5.9 %collective-permute-done.28.rest_6_ = bf16[576,384]{1,0:T(8,128)(2,1)} collective-permute-done((bf16[576,384]{1,0:T(8,128)(2,1)}, bf16[576,384]{1,0:T(8,128)(2,1)}, u32[]{:S(2)}, u32[]{:S(2)}) %collective-permute-start.28) | collective-permute-done | bytes 442400 | tf_op jit(solution)/shard_map/ppermute | solution.py:648
  78.1 5.9 %collective-permute-done.26.rest_4_ = bf16[576,384]{1,0:T(8,128)(2,1)} collective-permute-done((bf16[576,384]{1,0:T(8,128)(2,1)}, bf16[576,384]{1,0:T(8,128)(2,1)}, u32[]{:S(2)}, u32[]{:S(2)}) %collective-permute-start.26) | collective-permute-done | bytes 442400 | tf_op jit(solution)/shard_map/ppermute | solution.py:648
  89.6 7.6 %collective-permute-done.18.rest_6_ = bf16[512,512]{1,0:T(8,128)(2,1)} collective-permute-done((bf16[512,512]{1,0:T(8,128)(2,1)S(1)}, bf16[512,512]{1,0:T(8,128)(2,1)}, u32[]{:S(2)}, u32[]{:S(2)}) %collective-permute-start.18) | collective-permute-done | bytes 524320 | tf_op jit(solution)/shard_map/ppermute | solution.py:648
  97.2 8.5 %collective-permute-done.16.rest_4_ = bf16[512,512]{1,0:T(8,128)(2,1)} collective-permute-done((bf16[512,512]{1,0:T(8,128)(2,1)S(1)}, bf16[512,512]{1,0:T(8,128)(2,1)}, u32[]{:S(2)}, u32[]{:S(2)}) %collective-permute-start.16) | collective-permute-done | bytes 524320 | tf_op jit(solution)/shard_map/ppermute | solution.py:648
  110.5 8.2 %collective-permute-done.38.rest_6_ = bf16[512,512]{1,0:T(8,128)(2,1)S(1)} collective-permute-done((bf16[512,512]{1,0:T(8,128)(2,1)S(1)}, bf16[512,512]{1,0:T(8,128)(2,1)S(1)}, u32[]{:S(2)}, u32[]{:S(2)}) %collective-permute-start.38) | collective-permute-done | bytes 524320 | tf_op jit(solution)/shard_map/ppermute | solution.py:648
  123.1 23.3 %attn_forward.2 = (f32[1024,512]{1,0:T(8,128)}, bf16[1024,512]{1,0:T(8,128)(2,1)}, bf16[1024,128]{1,0:T(8,128)(2,1)}, f32[1024,512]{1,0:T(8,128)}, f32[1024,128]...) custom-call(s32[20]{0:T(128)} %pad_add_fusion.idx, ...), custom_call_target="tpu_custom_call" | custom-call | flops 8000000000 | bytes 14000000 | tf_op jit(solution)/shard_map/attn_forward/pallas_call | solution.py:544
  147.3 10.9 %ffn_forward.2.x_ref = f32[1024,512]{1,0:T(8,128)} custom-call(s32[20]{0:T(128)} %pad_add_fusion.idx, f32[1024,512]{1,0:T(8,128)} %get-tuple-element.73.x_ref, f32[8,512]{1,0:T(8,128)} %get-tuple-element.74.gains_ref, bf16[512,512]{1,0:T(8,128)(2,1)} %copy-done.34, bf16[512,512]{1,0:T(8,128)(2,1)} %collective-permute-done.13.rest_1_, ...), custom_call_target="tpu_custom_call" | custom-call | flops 5000000000 | bytes 8000000 | tf_op jit(solution)/shard_map/ffn_forward/pallas_call | solution.py:566
  159.4 23.7 %attn_forward.3 = (f32[1024,512]{1,0:T(8,128)}, bf16[1024,512]{1,0:T(8,128)(2,1)}, bf16[1024,128]{1,0:T(8,128)(2,1)}, f32[1024,512]{1,0:T(8,128)}, f32[1024,128]...) custom-call(s32[20]{0:T(128)} %pad_add_fusion.idx, ...), custom_call_target="tpu_custom_call" | custom-call | flops 8000000000 | bytes 14000000 | tf_op jit(solution)/shard_map/attn_forward/pallas_call | solution.py:544
  184.1 20.8 %ffn_backward.2 = (f32[1024,512]{1,0:T(8,128)}, f32[8,512]{1,0:T(8,128)}, bf16[4,4,128,512]{3,2,1,0:T(8,128)(2,1)}, bf16[4,4,128,512]{3,2,1,0:T(8,128)(2,1)}) custom-call(s32[20]{0:T(128)} %pad_add_fusion.idx, bf16[1024,512]{1,0:T(8,128)(2,1)} %up_ref.1, f32[1024,512]{1,0:T(8,128)} %get-tuple-element.75.x_ref, f32[8,512]{1,0:T(8,128)} %get-tuple-element.76.gains_ref, ...), custom_call_target="tpu_custom_call" | custom-call | flops 12999999488 | bytes 14000000 | tf_op jit(solution)/shard_map/ffn_backward/pallas_call | solution.py:578
  204.9 17.9 %output_backward.2 = (bf16[1024,512]{1,0:T(8,128)(2,1)}, f32[1024,128]{1,0:T(8,128)}, bf16[1024,128]{1,0:T(8,128)(2,1)}, bf16[4,4,64,384]{3,2,1,0:T(8,128)(2,1)}, bf16[4,4,64,384]{3,2,1,0:T(8,128)(2,1)}) custom-call(s32[20]{0:T(128)} %pad_add_fusion.idx, f32[1024,512]{1,0:T(8,128)} %get-tuple-element.77.mid_ref, f32[1024,8]{1,0:T(8,128)} %convert_element_type.693.hc_ref, ...), custom_call_target="tpu_custom_call" | custom-call | flops 5000000000 | bytes 16000000 | tf_op jit(solution)/shard_map/output_backward/pallas_call | solution.py:595
  222.8 28.8 %attn_backward.2 = (f32[1024,512]{1,0:T(8,128)}, bf16[4,4,80,384]{3,2,1,0:T(8,128)(2,1)}, bf16[4,4,80,384]{3,2,1,0:T(8,128)(2,1)}) custom-call(s32[20]{0:T(128)} %pad_add_fusion.idx, f32[1024,512]{1,0:T(8,128)} %get-tuple-element.77.mid_ref, f32[1024,512]{1,0:T(8,128)} %ffn_forward.2.x_ref, f32[1024,8]{1,0:T(8,128)} %convert_element_type.693.hc_ref, ...), custom_call_target="tpu_custom_call" | custom-call | flops 10000000000 | bytes 16000000 | tf_op jit(solution)/shard_map/attn_backward/pallas_call | solution.py:611
  251.6 20.9 %ffn_backward.3 = (f32[1024,512]{1,0:T(8,128)}, f32[8,512]{1,0:T(8,128)}, bf16[4,4,128,512]{3,2,1,0:T(8,128)(2,1)}, bf16[4,4,128,512]{3,2,1,0:T(8,128)(2,1)}) custom-call(s32[20]{0:T(128)} %pad_add_fusion.idx, f32[1024,512]{1,0:T(8,128)} %get-tuple-element.89.up_ref, f32[1024,512]{1,0:T(8,128)} %get-tuple-element.73.x_ref, ...), custom_call_target="tpu_custom_call" | custom-call | flops 12999999488 | bytes 14000000 | tf_op jit(solution)/shard_map/ffn_backward/pallas_call | solution.py:578
  272.5 17.9 %output_backward.3 = (bf16[1024,512]{1,0:T(8,128)(2,1)}, f32[1024,128]{1,0:T(8,128)}, bf16[1024,128]{1,0:T(8,128)(2,1)}, bf16[4,4,64,384]{3,2,1,0:T(8,128)(2,1)}, bf16[4,4,64,384]{3,2,1,0:T(8,128)(2,1)}) custom-call(s32[20]{0:T(128)} %pad_add_fusion.idx, f32[1024,512]{1,0:T(8,128)} %get-tuple-element.90.mid_ref, f32[1024,8]{1,0:T(8,128)} %convert_element_type.693.hc_ref, ...), custom_call_target="tpu_custom_call" | custom-call | flops 5000000000 | bytes 16000000 | tf_op jit(solution)/shard_map/output_backward/pallas_call | solution.py:595
  291.0 28.5 %attn_backward.3 = (f32[1024,512]{1,0:T(8,128)}, bf16[4,4,80,384]{3,2,1,0:T(8,128)(2,1)}, bf16[4,4,80,384]{3,2,1,0:T(8,128)(2,1)}) custom-call(s32[20]{0:T(128)} %pad_add_fusion.idx, f32[1024,512]{1,0:T(8,128)} %get-tuple-element.90.mid_ref, bf16[1024,512]{1,0:T(8,128)(2,1)} %x_ref.3, f32[1024,8]{1,0:T(8,128)} %convert_element_type.693.hc_ref, ...), custom_call_target="tpu_custom_call" | custom-call | flops 10000000000 | bytes 16000000 | tf_op jit(solution)/shard_map/attn_backward/pallas_call | solution.py:611
  320.1 10.8 %ffn_forward.3 = bf16[1024,512]{1,0:T(8,128)(2,1)} custom-call(s32[20]{0:T(128)} %pad_add_fusion.idx, f32[1024,512]{1,0:T(8,128)} %get-tuple-element.75.x_ref, f32[8,512]{1,0:T(8,128)} %get-tuple-element.76.gains_ref, bf16[512,512]{1,0:T(8,128)(2,1)} %copy-done.33, bf16[512,512]{1,0:T(8,128)(2,1)} %copy-done.39, bf16[512,512]{1,0:T(8,128)(2,1)} %copy-done.38, ...), custom_call_target="tpu_custom_call" | custom-call | flops 5000000000 | bytes 8000000 | tf_op jit(solution)/shard_map/ffn_forward/pallas_call | solution.py:566
  336.0 4.1 collective-permute-done.55
  365.4 4.1 collective-permute-done.41
  416.8 10.8 %collective-permute-done.71 = bf16[4,128,512]{2,1,0:T(8,128)(2,1)} collective-permute-done((bf16[4,128,512]{2,1,0:T(8,128)(2,1)}, bf16[4,128,512]{2,1,0:T(8,128)(2,1)}, u32[]{:S(2)}, u32[]{:S(2)}) %collective-permute-start.71) | collective-permute-done | bytes 524320 | tf_op jit(solution)/shard_map/ppermute | solution.py:658
  437.0 6.3 %collective-permute-done.78 = bf16[4,128,512]{2,1,0:T(8,128)(2,1)S(1)} collective-permute-done((bf16[4,128,512]{2,1,0:T(8,128)(2,1)S(1)}, bf16[4,128,512]{2,1,0:T(8,128)(2,1)S(1)}, u32[]{:S(2)}, u32[]{:S(2)}) %collective-permute-start.78) | collective-permute-done | bytes 524320 | tf_op jit(solution)/shard_map/ppermute | solution.py:658
  482.4 4.0 collective-permute-start.90
  (370 shorter events, 198.2 us)
Async XLA Ops:
  2.7 48.0 %collective-permute-start.12 = (bf16[128,512]{1,0:T(8,128)(2,1)S(1)}, bf16[128,512]{1,0:T(8,128)(2,1)S(1)}, u32[]{:S(2)}, u32[]{:S(2)}) collective-permute-start(bf16[128,512]{1,0:T(8,128)(2,1)S(1)} %pad_maximum_fusion.4), channel_id=1, source_target_pairs={{0,3},{1,0},{2,1},{3,2},{4,7},{5,4},{6,5},{7,6},{8,11},{9,8},{10,9... | collective-permute-start | bytes 393224 | tf_op jit(solution)/shard_map/ppermute | solution.py:646
  7.8 42.9 %collective-permute-start.11 = (bf16[128,512]{1,0:T(8,128)(2,1)S(1)}, bf16[128,512]{1,0:T(8,128)(2,1)S(1)}, u32[]{:S(2)}, u32[]{:S(2)}) collective-permute-start(bf16[128,512]{1,0:T(8,128)(2,1)S(1)} %pad_maximum_fusion.4), channel_id=1, source_target_pairs={{0,2},{1,3},{2,0},{3,1},{4,6},{5,7},{6,4},{7,5},{8,10},{9,11},{10,... | collective-permute-start | bytes 393224 | tf_op jit(solution)/shard_map/ppermute | solution.py:646
  13.6 27.9 %collective-permute-start.22 = (bf16[144,384]{1,0:T(8,128)(2,1)S(1)}, bf16[144,384]{1,0:T(8,128)(2,1)S(1)}, u32[]{:S(2)}, u32[]{:S(2)}) collective-permute-start(bf16[144,384]{1,0:T(8,128)(2,1)S(1)} %pad_maximum_fusion.7), channel_id=1, source_target_pairs={{0,3},{1,0},{2,1},{3,2},{4,7},{5,4},{6,5},{7,6},{8,11},{9,8},{10,9... | collective-permute-start | bytes 331784 | tf_op jit(solution)/shard_map/ppermute | solution.py:646
  14.1 25.7 %collective-permute-start.20 = (bf16[144,384]{1,0:T(8,128)(2,1)S(1)}, bf16[144,384]{1,0:T(8,128)(2,1)S(1)}, u32[]{:S(2)}, u32[]{:S(2)}) collective-permute-start(bf16[144,384]{1,0:T(8,128)(2,1)S(1)} %pad_maximum_fusion.7), channel_id=1, source_target_pairs={{0,1},{1,2},{2,3},{3,0},{4,5},{5,6},{6,7},{7,4},{8,9},{9,10},{10,1... | collective-permute-start | bytes 331784 | tf_op jit(solution)/shard_map/ppermute | solution.py:646
  67.2 30.0 %collective-permute-start.18 = (bf16[512,512]{1,0:T(8,128)(2,1)S(1)}, bf16[512,512]{1,0:T(8,128)(2,1)}, u32[]{:S(2)}, u32[]{:S(2)}) collective-permute-start(bf16[512,512]{1,0:T(8,128)(2,1)S(1)} %constant_dynamic-update-slice_fusion.6.rest_0_), channel_id=1, source_target_pairs={{0,24},{4,28},{8,16},{12,20},{16,8},{20,12},{24,0},{28,4},{1,25},{... | collective-permute-start | bytes 1572872 | tf_op jit(solution)/shard_map/ppermute | solution.py:648
  76.4 29.2 %collective-permute-start.16 = (bf16[512,512]{1,0:T(8,128)(2,1)S(1)}, bf16[512,512]{1,0:T(8,128)(2,1)}, u32[]{:S(2)}, u32[]{:S(2)}) collective-permute-start(bf16[512,512]{1,0:T(8,128)(2,1)S(1)} %constant_dynamic-update-slice_fusion.6.rest_0_), channel_id=1, source_target_pairs={{0,16},{4,20},{8,24},{12,28},{16,0},{20,4},{24,8},{28,12},{1,17},{... | collective-permute-start | bytes 1572872 | tf_op jit(solution)/shard_map/ppermute | solution.py:648
  86.8 32.0 %collective-permute-start.38 = (bf16[512,512]{1,0:T(8,128)(2,1)S(1)}, bf16[512,512]{1,0:T(8,128)(2,1)S(1)}, u32[]{:S(2)}, u32[]{:S(2)}) collective-permute-start(bf16[512,512]{1,0:T(8,128)(2,1)S(1)} %constant_dynamic-update-slice_fusion.17.rest_0_), channel_id=1, source_target_pairs={{0,24},{4,28},{8,16},{12,20},{16,8},{20,12},{24,0},{28,4},{1,25},{... | collective-permute-start | bytes 1572872 | tf_op jit(solution)/shard_map/ppermute | solution.py:648
  109.3 48.9 %collective-permute-start.36 = (bf16[512,512]{1,0:T(8,128)(2,1)S(1)}, bf16[512,512]{1,0:T(8,128)(2,1)S(1)}, u32[]{:S(2)}, u32[]{:S(2)}) collective-permute-start(bf16[512,512]{1,0:T(8,128)(2,1)S(1)} %constant_dynamic-update-slice_fusion.17.rest_0_), channel_id=1, source_target_pairs={{0,16},{4,20},{8,24},{12,28},{16,0},{20,4},{24,8},{28,12},{1,17},{... | collective-permute-start | bytes 1572872 | tf_op jit(solution)/shard_map/ppermute | solution.py:648
  118.8 39.7 %collective-permute-start.34 = (bf16[512,512]{1,0:T(8,128)(2,1)S(1)}, bf16[512,512]{1,0:T(8,128)(2,1)S(1)}, u32[]{:S(2)}, u32[]{:S(2)}) collective-permute-start(bf16[512,512]{1,0:T(8,128)(2,1)S(1)} %constant_dynamic-update-slice_fusion.17.rest_0_), channel_id=1, source_target_pairs={{0,8},{4,12},{8,0},{12,4},{16,24},{20,28},{24,16},{28,20},{1,9},{5... | collective-permute-start | bytes 1572872 | tf_op jit(solution)/shard_map/ppermute | solution.py:648
  120.8 25.6 %collective-permute-start.19 = (bf16[512,512]{1,0:T(8,128)(2,1)}, bf16[512,512]{1,0:T(8,128)(2,1)}, u32[]{:S(2)}, u32[]{:S(2)}) collective-permute-start(bf16[512,512]{1,0:T(8,128)(2,1)} %collective-permute-done.18.rest_6_), channel_id=1, source_target_pairs={{0,4},{4,0},{8,12},{12,8},{16,20},{20,16},{24,28},{28,24},{1,5},{5... | collective-permute-start | bytes 1572872 | tf_op jit(solution)/shard_map/ppermute | solution.py:649
  120.8 26.0 %collective-permute-start.17 = (bf16[512,512]{1,0:T(8,128)(2,1)}, bf16[512,512]{1,0:T(8,128)(2,1)}, u32[]{:S(2)}, u32[]{:S(2)}) collective-permute-start(bf16[512,512]{1,0:T(8,128)(2,1)} %collective-permute-done.16.rest_4_), channel_id=1, source_target_pairs={{0,4},{4,0},{8,12},{12,8},{16,20},{20,16},{24,28},{28,24},{1,5},{5... | collective-permute-start | bytes 1572872 | tf_op jit(solution)/shard_map/ppermute | solution.py:649
  121.3 25.7 %collective-permute-start.15 = (bf16[512,512]{1,0:T(8,128)(2,1)}, bf16[512,512]{1,0:T(8,128)(2,1)}, u32[]{:S(2)}, u32[]{:S(2)}) collective-permute-start(bf16[512,512]{1,0:T(8,128)(2,1)} %collective-permute-done.14.rest_2_), channel_id=1, source_target_pairs={{0,4},{4,0},{8,12},{12,8},{16,20},{20,16},{24,28},{28,24},{1,5},{5... | collective-permute-start | bytes 1572872 | tf_op jit(solution)/shard_map/ppermute | solution.py:649
  158.2 24.9 %collective-permute-start.33 = (bf16[512,512]{1,0:T(8,128)(2,1)S(1)}, bf16[512,512]{1,0:T(8,128)(2,1)S(1)}, u32[]{:S(2)}, u32[]{:S(2)}) collective-permute-start(bf16[512,512]{1,0:T(8,128)(2,1)S(1)} %constant_dynamic-update-slice_fusion.17.rest_0_), channel_id=1, source_target_pairs={{0,4},{4,0},{8,12},{12,8},{16,20},{20,16},{24,28},{28,24},{1,5},{5... | collective-permute-start | bytes 1572872 | tf_op jit(solution)/shard_map/ppermute | solution.py:649
  290.4 40.5 %collective-permute-start.54 = (bf16[4,4,64,384]{3,2,1,0:T(8,128)(2,1)}, bf16[4,4,64,384]{3,2,1,0:T(8,128)(2,1)}, u32[]{:S(2)}, u32[]{:S(2)}) collective-permute-start(bf16[4,4,64,384]{3,2,1,0:T(8,128)(2,1)} %get-tuple-element.108), channel_id=1, source_target_pairs={{0,4},{4,0},{8,12},{12,8},{16,20},{20,16},{24,28},{28,24},{1,5},{5... | collective-permute-start | bytes 2359304 | tf_op jit(solution)/shard_map/ppermute | solution.py:654
  290.6 42.1 %collective-permute-start.61 = (bf16[4,4,64,384]{3,2,1,0:T(8,128)(2,1)}, bf16[4,4,64,384]{3,2,1,0:T(8,128)(2,1)S(1)}, u32[]{:S(2)}, u32[]{:S(2)}) collective-permute-start(bf16[4,4,64,384]{3,2,1,0:T(8,128)(2,1)} %get-tuple-element.110), channel_id=1, source_target_pairs={{0,4},{4,0},{8,12},{12,8},{16,20},{20,16},{24,28},{28,24},{1,5},{5... | collective-permute-start | bytes 2359304 | tf_op jit(solution)/shard_map/ppermute | solution.py:654
  319.5 35.6 %collective-permute-start.40 = (bf16[4,4,80,384]{3,2,1,0:T(8,128)(2,1)}, bf16[4,4,80,384]{3,2,1,0:T(8,128)(2,1)S(1)}, u32[]{:S(2)}, u32[]{:S(2)}) collective-permute-start(bf16[4,4,80,384]{3,2,1,0:T(8,128)(2,1)} %get-tuple-element.104), channel_id=1, source_target_pairs={{0,4},{4,0},{8,12},{12,8},{16,20},{20,16},{24,28},{28,24},{1,5},{5... | collective-permute-start | bytes 2949128 | tf_op jit(solution)/shard_map/ppermute | solution.py:654
  319.7 38.2 %collective-permute-start.47 = (bf16[4,4,80,384]{3,2,1,0:T(8,128)(2,1)}, bf16[4,4,80,384]{3,2,1,0:T(8,128)(2,1)S(1)}, u32[]{:S(2)}, u32[]{:S(2)}) collective-permute-start(bf16[4,4,80,384]{3,2,1,0:T(8,128)(2,1)} %get-tuple-element.106), channel_id=1, source_target_pairs={{0,4},{4,0},{8,12},{12,8},{16,20},{20,16},{24,28},{28,24},{1,5},{5... | collective-permute-start | bytes 2949128 | tf_op jit(solution)/shard_map/ppermute | solution.py:654
  364.2 34.0 %collective-permute-start.68 = (bf16[4,4,128,512]{3,2,1,0:T(8,128)(2,1)S(1)}, bf16[4,4,128,512]{3,2,1,0:T(8,128)(2,1)S(1)}, u32[]{:S(2)}, u32[]{:S(2)}) collective-permute-start(bf16[4,4,128,512]{3,2,1,0:T(8,128)(2,1)S(1)} %copy-done.35), channel_id=1, source_target_pairs={{0,4},{4,0},{8,12},{12,8},{16,20},{20,16},{24,28},{28,24},{1,5},{5... | collective-permute-start | bytes 6291464 | tf_op jit(solution)/shard_map/ppermute | solution.py:654
  364.3 43.3 %collective-permute-start.75 = (bf16[4,4,128,512]{3,2,1,0:T(8,128)(2,1)}, bf16[4,4,128,512]{3,2,1,0:T(8,128)(2,1)}, u32[]{:S(2)}, u32[]{:S(2)}) collective-permute-start(bf16[4,4,128,512]{3,2,1,0:T(8,128)(2,1)} %get-tuple-element.114), channel_id=1, source_target_pairs={{0,4},{4,0},{8,12},{12,8},{16,20},{20,16},{24,28},{28,24},{1,5},{5... | collective-permute-start | bytes 6291464 | tf_op jit(solution)/shard_map/ppermute | solution.py:654
  401.0 26.6 %collective-permute-start.71 = (bf16[4,128,512]{2,1,0:T(8,128)(2,1)}, bf16[4,128,512]{2,1,0:T(8,128)(2,1)}, u32[]{:S(2)}, u32[]{:S(2)}) collective-permute-start(bf16[4,128,512]{2,1,0:T(8,128)(2,1)} %get-tuple-element.144), channel_id=1, source_target_pairs={{0,24},{4,28},{8,16},{12,20},{16,8},{20,12},{24,0},{28,4},{1,25},{... | collective-permute-start | bytes 1572872 | tf_op jit(solution)/shard_map/ppermute | solution.py:658
  403.1 26.4 %collective-permute-start.70 = (bf16[4,128,512]{2,1,0:T(8,128)(2,1)}, bf16[4,128,512]{2,1,0:T(8,128)(2,1)}, u32[]{:S(2)}, u32[]{:S(2)}) collective-permute-start(bf16[4,128,512]{2,1,0:T(8,128)(2,1)} %get-tuple-element.145), channel_id=1, source_target_pairs={{0,16},{4,20},{8,24},{12,28},{16,0},{20,4},{24,8},{28,12},{1,17},{... | collective-permute-start | bytes 1572872 | tf_op jit(solution)/shard_map/ppermute | solution.py:658
  409.5 27.4 %collective-permute-start.76 = (bf16[4,128,512]{2,1,0:T(8,128)(2,1)S(1)}, bf16[4,128,512]{2,1,0:T(8,128)(2,1)S(1)}, u32[]{:S(2)}, u32[]{:S(2)}) collective-permute-start(bf16[4,128,512]{2,1,0:T(8,128)(2,1)S(1)} %get-tuple-element.146), channel_id=1, source_target_pairs={{0,8},{4,12},{8,0},{12,4},{16,24},{20,28},{24,16},{28,20},{1,9},{5... | collective-permute-start | bytes 1572872 | tf_op jit(solution)/shard_map/ppermute | solution.py:658
  410.4 32.9 %collective-permute-start.78 = (bf16[4,128,512]{2,1,0:T(8,128)(2,1)S(1)}, bf16[4,128,512]{2,1,0:T(8,128)(2,1)S(1)}, u32[]{:S(2)}, u32[]{:S(2)}) collective-permute-start(bf16[4,128,512]{2,1,0:T(8,128)(2,1)S(1)} %get-tuple-element.147), channel_id=1, source_target_pairs={{0,24},{4,28},{8,16},{12,20},{16,8},{20,12},{24,0},{28,4},{1,25},{... | collective-permute-start | bytes 1572872 | tf_op jit(solution)/shard_map/ppermute | solution.py:658
  415.3 29.3 %collective-permute-start.77 = (bf16[4,128,512]{2,1,0:T(8,128)(2,1)S(1)}, bf16[4,128,512]{2,1,0:T(8,128)(2,1)S(1)}, u32[]{:S(2)}, u32[]{:S(2)}) collective-permute-start(bf16[4,128,512]{2,1,0:T(8,128)(2,1)S(1)} %get-tuple-element.148), channel_id=1, source_target_pairs={{0,16},{4,20},{8,24},{12,28},{16,0},{20,4},{24,8},{28,12},{1,17},{... | collective-permute-start | bytes 1572872 | tf_op jit(solution)/shard_map/ppermute | solution.py:658
  (113 other events, 2026.6 us)
